TPU v7x, 256 devices: a whole 4x4x8 slice. The times are simulated.
256 devices in a mesh: group: 8 (over y_hi, x), shard: 32 (over y_lo, z, core).
Axes of the slice: x: 4, y: 4 (y_hi: 2, y_lo: 2; y = y_hi * 2 + y_lo), z: 8, core: 2. Of those that a mesh axis runs over, the one named last changes fastest.
Arguments:
- entity_rows: float32 [262144, 200], P(('group', 'shard')), may hold values from -4 to 4
- entity_state: float32 [262144], P(('group', 'shard')), may hold values from 0.5 to 4
- relation_rows: float32 [1387, 200], replicated, may hold values from -6 to 6
- relation_state: float32 [1387], replicated, may hold values from 16 to 160
- conv_weight: bfloat16 [32, 3, 3], replicated, may hold values from -2 to 2
- conv_bias: float32 [32], replicated, may hold values from -3 to 3
- fc_weight: bfloat16 [10368, 200], replicated, may hold values from -0.0625 to 0.0625
- fc_bias: float32 [200], replicated, may hold values from -3 to 3
- head_ids: int32 [2, 32768], P(None, ('group', 'shard')), may hold values from 0 to 1023
- rel_ids: int32 [2, 32768], P(None, ('group', 'shard')), may hold values from 0 to 1386
- tail_ids: int32 [2, 32768], P(None, ('group', 'shard')), may hold values from 0 to 1023
- neg_ids: int32 [2, 8192], P(None, ('group', 'shard')), may hold values from 0 to 1023
Outputs:
- new_entity_rows: float32 [262144, 200], P(('group', 'shard'))
- new_entity_state: float32 [262144], P(('group', 'shard'))
- new_relation_rows: float32 [1387, 200], replicated
- new_relation_state: float32 [1387], replicated
All inputs are finite; a program needn't handle non-finite values.
Results may differ from a plain program's by a relative error of at most 0.002.
Values may be sent and summed in bfloat16 or wider, within the bound.
A program may use at most 128 MiB of HBM per device.

v0:
```python
import jax
import jax.numpy as jnp
from jax import lax
from jax.sharding import PartitionSpec as P

EMB_H = 10
EMB_W = 20
D = 200
FILTERS = 32
FLAT = 10368
REL = 1387
ROUNDS = 2


negative_weight = 0.03125
learn_rate = 0.5


def from_partner(block, axis, bit):
    count = lax.axis_size(axis)
    route = []
    for low in range(count):
        high = low | 1 << bit
        if high != low and high < count:
            route += [(low, high), (high, low)]
    return lax.ppermute(block, axis, route)


def silu_slope(values):
    sigma = jax.nn.sigmoid(values)
    return sigma * (1.0 + values * (1.0 - sigma))


def adagrad(rows, state, gradient):
    state = state + jnp.mean(gradient * gradient, axis=1)
    rows = rows - learn_rate * gradient / jnp.sqrt(state)[:, None]
    return (rows, state)


def local_pass(head_rows, rel_rows, tail_rows, negset, conv_weight, conv_bias, fc_weight, fc_bias):
    number = head_rows.shape[0]
    picture = jnp.concatenate(
        [head_rows.reshape(number, EMB_H, EMB_W), rel_rows.reshape(number, EMB_H, EMB_W)], axis=1
    )
    picture = jnp.transpose(picture, (1, 2, 0))
    height = picture.shape[0] - 2
    across = picture.shape[1] - 2
    patches = jnp.stack(
        [
            picture[row_off : row_off + height, col_off : col_off + across]
            for row_off in range(3)
            for col_off in range(3)
        ]
    )
    filters = conv_weight.reshape(FILTERS, 9)
    pre1 = (
        jnp.einsum("fk,kijt->fijt", filters, patches, preferred_element_type=jnp.float32)
        + conv_bias[:, None, None, None]
    )
    act = jax.nn.silu(pre1).astype(jnp.bfloat16).reshape(FLAT, number)
    pre2 = (
        lax.dot_general(
            fc_weight, act, (((0,), (0,)), ((), ())), preferred_element_type=jnp.float32
        )
        + fc_bias[:, None]
    )
    query = jax.nn.silu(pre2).astype(jnp.bfloat16)
    tail_cols = tail_rows.T.astype(jnp.float32)
    pos_score = jnp.sum(query.astype(jnp.float32) * tail_cols, axis=0)
    neg_score = jnp.dot(negset, query, preferred_element_type=jnp.float32)
    pos_grad = -jax.nn.sigmoid(-pos_score)
    neg_grad = (negative_weight * jax.nn.sigmoid(neg_score)).astype(jnp.bfloat16)
    query_grad = pos_grad[None, :] * tail_cols + lax.dot_general(
        negset, neg_grad, (((0,), (0,)), ((), ())), preferred_element_type=jnp.float32
    )
    pre2_grad = (query_grad * silu_slope(pre2)).astype(jnp.bfloat16)
    act_grad = jnp.dot(fc_weight, pre2_grad, preferred_element_type=jnp.float32)
    pre1_grad = (act_grad.reshape(pre1.shape) * silu_slope(pre1)).astype(jnp.bfloat16)
    spread = jnp.einsum("fk,fijt->kijt", filters, pre1_grad, preferred_element_type=jnp.float32)
    picture_grad = jnp.zeros((height + 2, across + 2, number), jnp.float32)
    for offset in range(9):
        row_off, col_off = divmod(offset, 3)
        picture_grad = picture_grad + jnp.pad(
            spread[offset], ((row_off, 2 - row_off), (col_off, 2 - col_off), (0, 0))
        )
    head_grad = jnp.transpose(picture_grad[:EMB_H], (2, 0, 1)).reshape(number, D)
    relation_grad = jnp.transpose(picture_grad[EMB_H:], (2, 0, 1)).reshape(number, D)
    tail_grad = (pos_grad[None, :] * query.astype(jnp.float32)).T
    return (head_grad, relation_grad, tail_grad, neg_grad, query)


def shards(
    entity_rows,
    entity_state,
    relation_rows,
    relation_state,
    conv_weight,
    conv_bias,
    fc_weight,
    fc_bias,
    head_ids,
    rel_ids,
    tail_ids,
    neg_ids,
):
    ent_rows_dev = entity_rows.shape[0]
    for round_index in range(ROUNDS):
        ent_bf = entity_rows.astype(jnp.bfloat16)
        rel_bf = relation_rows.astype(jnp.bfloat16)
        heads = head_ids[round_index]
        relations = rel_ids[round_index]
        tails = tail_ids[round_index]
        negatives = neg_ids[round_index]
        partner_rows = from_partner(ent_bf, "group", round_index)
        tail_rows = partner_rows[tails]
        own_negative = partner_rows[negatives]
        negset = lax.all_gather(own_negative, "shard", axis=0, tiled=True)
        head_grad, relation_grad, tail_grad, neg_grad, query = local_pass(
            ent_bf[heads],
            rel_bf[relations],
            tail_rows,
            negset,
            conv_weight,
            conv_bias,
            fc_weight,
            fc_bias,
        )
        my_share = lax.psum_scatter(
            lax.dot_general(
                neg_grad, query, (((1,), (1,)), ((), ())), preferred_element_type=jnp.float32
            ),
            "shard",
            scatter_dimension=0,
            tiled=True,
        )
        gradient = jax.ops.segment_sum(head_grad, heads, num_segments=ent_rows_dev)
        outgoing = jax.ops.segment_sum(
            tail_grad, tails, num_segments=ent_rows_dev
        ) + jax.ops.segment_sum(my_share, negatives, num_segments=ent_rows_dev)
        gradient = gradient + from_partner(outgoing, "group", round_index)
        rel_part = jax.ops.segment_sum(relation_grad, relations, num_segments=REL)
        entity_rows, entity_state = adagrad(entity_rows, entity_state, gradient)
        rel_total = lax.psum(rel_part, ("group", "shard"))
        relation_rows, relation_state = adagrad(relation_rows, relation_state, rel_total)
    return (entity_rows, entity_state, relation_rows, relation_state)


def solution(mesh):
    in_specs = (
        P(("group", "shard"), None),
        P(("group", "shard")),
        P(),
        P(),
        P(),
        P(),
        P(),
        P(),
        P(None, ("group", "shard")),
        P(None, ("group", "shard")),
        P(None, ("group", "shard")),
        P(None, ("group", "shard")),
    )
    out_specs = (P(("group", "shard"), None), P(("group", "shard")), P(), P())
    return jax.shard_map(shards, mesh=mesh, in_specs=in_specs, out_specs=out_specs, check_vma=False)
```

profile of v0, /device:TPU:1, one launch (start us, length us, event | category | flops | bytes accessed | tf_op | source)
XLA Modules:
  0.0 818.9 jit_solution(13270285148101212783)
XLA Ops:
  8.1 1.6 copy.744
  10.5 2.0 collective-permute-start
  12.6 1.7 copy.747
  16.0 1.9 gather_fusion
  19.2 2.0 gather_fusion.1
  24.7 8.3 %stack.69 = bf16[9,18,18,128]{3,0,2,1:T(8,128)(2,1)} concatenate(bf16[1,18,18,128]{3,0,2,1:T(2,128)(2,1)S(1)} %copy.718, bf16[1,18,18,128]{3,0,2,1:T(2,128)(2,1)S(1)} %copy.719, bf16[1,18,18,128]{3,0,2,1:T(2,128)(2,1)S(1)} %copy.720, bf16[1,18,18,128]{3,0,2,1:T(2,128)(2,1)S(1)} %copy.721, bf16[1,18,18,128]{3,0,2,1:T(2,128)(2,1)S(1)} %copy.722, ...), dimensions={0} | concatenate | bytes 1492992 | tf_op jit(solution)/shard_map/stack | solution.py:48
  33.0 5.1 fusion.11
  38.2 2.9 copy.727
  41.0 5.5 reshape.293
  48.3 1.9 gather_fusion.2
  50.3 1.7 gather_fusion.3
  52.0 39.4 %all-gather = bf16[1024,200]{1,0:T(8,128)(2,1)S(1)} all-gather(bf16[32,200]{1,0:T(8,128)(2,1)S(1)} %gather_fusion.3), channel_id=2, replica_groups=mesh['group'=8,'shard'=32] {'shard'}, dimensions={0}, use_global_device_ids=true | all-gather | bytes 422400 | tf_op jit(solution)/shard_map/all_gather | solution.py:117
  91.4 4.3 fusion.54
  97.3 5.7 convolution_bitcast_fusion.1
  103.1 6.0 copy.732
  109.1 6.7 reshape.294
  116.1 5.9 fusion.23
  123.6 2.4 scatter_custom_fusion.2
  127.5 98.5 %reduce-scatter.7.cloned.1.call-done = f32[32,200]{1,0:T(8,128)} async-done(((f32[1024,200]{1,0:T(8,128)}), f32[32,200]{1,0:T(8,128)}) %reduce-scatter.7.cloned.1.call-update) | async-done | bytes 25616
  227.7 2.1 scatter_custom_fusion
  232.1 148.2 %all-reduce.21.cloned.1.call-done = f32[1387,200]{1,0:T(8,128)} async-done(((f32[1387,200]{1,0:T(8,128)}), f32[1387,200]{1,0:T(8,128)}) %all-reduce.21.cloned.1.call-update) | async-done | bytes 1109616 | tf_op jit(solution)/shard_map/psum | solution.py:143
  380.2 1.6 multiply_reduce_fusion.1
  381.9 1.6 fusion.91
  385.1 1.5 copy.742
  386.6 2.1 scatter_fusion
  391.1 2.7 collective-permute-start.2
  393.8 2.6 gather_fusion.4
  396.5 1.6 copy.745
  398.0 1.4 reshape.296
  407.6 8.6 %stack.79 = bf16[9,18,18,128]{3,0,2,1:T(8,128)(2,1)} concatenate(bf16[1,18,18,128]{3,0,2,1:T(2,128)(2,1)} %copy.749, bf16[1,18,18,128]{3,0,2,1:T(2,128)(2,1)} %copy.750, bf16[1,18,18,128]{3,0,2,1:T(2,128)(2,1)} %copy.751, bf16[1,18,18,128]{3,0,2,1:T(2,128)(2,1)} %copy.752, bf16[1,18,18,128]{3,0,2,1:T(2,128)(2,1)} %copy.753, bf16[1,18,18,128]{3,0,2,1:T(2,128)(2,1)} %copy.754, ...), dimensions={0} | concatenate | bytes 1492992 | tf_op jit(solution)/shard_map/stack | solution.py:48
  416.3 5.1 fusion.3
  421.4 2.9 copy.758
  424.3 5.5 reshape.299
  429.8 2.5 gather_fusion.6
  432.3 1.6 copy.759
  433.8 1.8 gather_fusion.7
  435.7 45.0 %all-gather.1 = bf16[1024,200]{1,0:T(8,128)(2,1)S(1)} all-gather(bf16[32,200]{1,0:T(8,128)(2,1)S(1)} %gather_fusion.7), channel_id=3, replica_groups=mesh['group'=8,'shard'=32] {'shard'}, dimensions={0}, use_global_device_ids=true | all-gather | bytes 422400 | tf_op jit(solution)/shard_map/all_gather | solution.py:117
  480.7 5.1 fusion.44
  487.4 6.0 convolution_bitcast_fusion
  493.4 6.0 copy.763
  499.4 6.7 reshape.300
  506.2 5.9 fusion.20
  514.2 1.6 reshape.411
  515.8 1.6 copy.775
  517.4 2.8 scatter_custom_fusion.5
  520.3 2.2 fusion.103
  523.8 1.6 reshape.403
  525.3 1.6 copy.774
  527.0 1.6 convert_multiply_fusion
  528.5 245.2 %all-reduce.23.cloned.1.call-done = f32[1387,200]{1,0:T(8,128)} async-done(((f32[1387,200]{1,0:T(8,128)}), f32[1387,200]{1,0:T(8,128)}) %all-reduce.23.cloned.1.call-update) | async-done | bytes 1109616 | tf_op jit(solution)/shard_map/psum | solution.py:143
  773.7 1.6 multiply_reduce_fusion
  775.4 1.5 copy.784
  776.9 1.6 pad_maximum_fusion.1
  778.5 1.7 copy.761
  780.2 2.8 scatter_custom_fusion.3
  783.0 2.4 copy.762
  785.4 2.7 collective-permute-start.3
  788.8 3.3 divide_subtract_fusion
  792.1 2.8 copy.777
  794.9 8.6 %collective-permute-done.3 = f32[1024,200]{0,1:T(8,128)} collective-permute-done((f32[1024,200]{0,1:T(8,128)}, f32[1024,200]{0,1:T(8,128)}, u32[]{:S(2)}, u32[]{:S(2)}) %collective-permute-start.3) | collective-permute-done | bytes 819232 | tf_op jit(solution)/shard_map/ppermute | solution.py:26
  803.5 1.5 copy.773
  805.0 1.7 scatter_fusion.1
  807.5 1.3 divide_subtract_fusion.2
  808.8 2.4 copy.776
  (161 shorter events, 36.6 us)
Async XLA Ops:
  8.0 4.5 copy-start
  8.0 6.3 copy-start.16
  8.0 6.9 copy-start.17
  8.0 7.4 copy-start.19
  8.0 10.0 %copy-start.18 = (s32[2,128]{1,0:T(2,128)S(1)}, s32[2,128]{1,0:T(2,128)}, u32[]{:S(2)}) copy-start(s32[2,128]{1,0:T(2,128)} %param.21) | copy-start | bytes 3076
  8.1 218.0 %reduce-scatter.7.cloned.1.call-start = ((), (), s32[]{:S(2)}) async-start(), calls=%async_computation.4 | async-start | bytes 1081344
  10.5 37.8 %collective-permute-start = (bf16[1024,200]{1,0:T(8,128)(2,1)}, bf16[1024,200]{1,0:T(8,128)(2,1)}, u32[]{:S(2)}, u32[]{:S(2)}) collective-permute-start(bf16[1024,200]{1,0:T(8,128)(2,1)} %convert_element_type.101), channel_id=1, source_target_pairs={{0,32},{32,0},{64,96},{96,64},{128,160},{160,128},{192,224},{224,1... | collective-permute-start | bytes 1228808 | tf_op jit(solution)/shard_map/ppermute | solution.py:26
  14.3 10.4 %copy-start.20 = (bf16[32,3,3]{0,2,1:T(4,128)(2,1)S(1)}, bf16[32,3,3]{0,2,1:T(4,128)(2,1)}, u32[]{:S(2)}) copy-start(bf16[32,3,3]{0,2,1:T(4,128)(2,1)} %param.16) | copy-start | bytes 1732
  19.2 13.8 %copy-start.23 = (f32[32]{0:T(128)S(1)}, f32[32]{0:T(128)}, u32[]{:S(2)}) copy-start(f32[32]{0:T(128)} %param.17) | copy-start | bytes 388
  24.7 91.4 %copy-start.13 = (bf16[32,9,1,1]{0,1,2,3:T(8,128)(2,1)}, bf16[32,9,1,1]{0,1,2,3:T(8,128)(2,1)S(1)}, u32[]{:S(2)}) copy-start(bf16[32,9,1,1]{0,1,2,3:T(8,128)(2,1)S(1)} %reshape.421) | copy-start | bytes 1732
  41.0 50.4 %copy-start.12 = (f32[200]{0:T(256)S(1)}, f32[200]{0:T(256)}, u32[]{:S(2)}) copy-start(f32[200]{0:T(256)} %param.19) | copy-start | bytes 2404
  115.8 264.5 %all-reduce.21.cloned.1.call-start = ((), (), s32[]{:S(2)}) async-start(), calls=%async_computation.2 | async-start | bytes 2850816 | tf_op jit(solution)/shard_map/psum | solution.py:143
  123.6 258.2 %copy-start.8 = (f32[1387]{0:T(1024)S(1)}, f32[1387]{0:T(1024)}, u32[]{:S(2)}) copy-start(f32[1387]{0:T(1024)} %param.15) | copy-start | bytes 16648
  126.1 647.6 %all-reduce.23.cloned.1.call-start = ((), (), s32[]{:S(2)}) async-start(), calls=%async_computation.3 | async-start | bytes 2850816 | tf_op jit(solution)/shard_map/psum | solution.py:143
  231.0 154.1 %collective-permute-start.1 = (f32[1024,200]{0,1:T(8,128)}, f32[1024,200]{0,1:T(8,128)}, u32[]{:S(2)}, u32[]{:S(2)}) collective-permute-start(f32[1024,200]{0,1:T(8,128)} %copy.731), channel_id=1, source_target_pairs={{0,32},{32,0},{64,96},{96,64},{128,160},{160,128},{192,224},{224,1... | collective-permute-start | bytes 2457608 | tf_op jit(solution)/shard_map/ppermute | solution.py:26
  381.9 7.6 copy-start.10
  388.9 0.6 copy-start.4
  389.5 0.6 copy-start.6
  391.1 38.7 %collective-permute-start.2 = (bf16[1024,200]{1,0:T(8,128)(2,1)}, bf16[1024,200]{1,0:T(8,128)(2,1)}, u32[]{:S(2)}, u32[]{:S(2)}) collective-permute-start(bf16[1024,200]{1,0:T(8,128)(2,1)} %fusion.90), channel_id=1, source_target_pairs={{0,64},{64,0},{32,96},{96,32},{128,192},{192,128},{160,224},{224,1... | collective-permute-start | bytes 1228808 | tf_op jit(solution)/shard_map/ppermute | solution.py:26
  393.8 22.4 %copy-start.14 = (bf16[32,9,1,1]{0,1,2,3:T(8,128)(2,1)S(1)}, bf16[32,9,1,1]{0,1,2,3:T(8,128)(2,1)}, u32[]{:S(2)}) copy-start(bf16[32,9,1,1]{0,1,2,3:T(8,128)(2,1)} %copy-done.13) | copy-start | bytes 1732
  393.8 22.4 %copy-start.24 = (f32[32]{0:T(128)S(1)}, f32[32]{0:T(128)}, u32[]{:S(2)}) copy-start(f32[32]{0:T(128)} %param.17) | copy-start | bytes 388
  480.7 6.7 copy-start.1
  485.8 0.6 copy-start.3
  499.4 6.7 copy-start.15
  499.4 6.7 copy-start.25
  513.3 9.3 %copy-start.22 = (s32[128,1]{0,1:T(1,128)S(1)}, s32[128,1]{0,1:T(1,128)}, u32[]{:S(2)}) copy-start(s32[128,1]{0,1:T(1,128)} %get-tuple-element.117) | copy-start | bytes 1540
  520.2 267.9 %copy-start.9 = (f32[1387]{0:T(1024)S(1)}, f32[1387]{0:T(1024)}, u32[]{:S(2)}) copy-start(f32[1387]{0:T(1024)} %param.15) | copy-start | bytes 16648
  520.3 255.1 %reduce-scatter.9.cloned.1.call-start = ((), (), s32[]{:S(2)}) async-start(), calls=%async_computation.5 | async-start | bytes 1081344
  785.4 18.0 %collective-permute-start.3 = (f32[1024,200]{0,1:T(8,128)}, f32[1024,200]{0,1:T(8,128)}, u32[]{:S(2)}, u32[]{:S(2)}) collective-permute-start(f32[1024,200]{0,1:T(8,128)} %copy.762), channel_id=1, source_target_pairs={{0,64},{64,0},{32,96},{96,32},{128,192},{192,128},{160,224},{224,1... | collective-permute-start | bytes 2457608 | tf_op jit(solution)/shard_map/ppermute | solution.py:26
  788.8 16.2 %copy-start.21 = (s32[128]{0:T(128)S(1)}, s32[128]{0:T(128)}, u32[]{:S(2)}) copy-start(s32[128]{0:T(128)} %get-tuple-element.106) | copy-start | bytes 1540
  792.1 12.9 %copy-start.2 = (f32[128,200]{1,0:T(8,128)S(1)}, f32[128,200]{1,0:T(8,128)}, u32[]{:S(2)}) copy-start(f32[128,200]{1,0:T(8,128)} %copy.774) | copy-start | bytes 307204
  792.1 14.8 %copy-start.5 = (f32[1024]{0:T(1024)S(1)}, f32[1024]{0:T(1024)}, u32[]{:S(2)}) copy-start(f32[1024]{0:T(1024)} %copy-done.4) | copy-start | bytes 12292
  792.1 14.8 %copy-start.11 = (f32[1024]{0:T(1024)S(1)}, f32[1024]{0:T(1024)}, u32[]{:S(2)}) copy-start(f32[1024]{0:T(1024)} %param.13) | copy-start | bytes 12292
  792.1 15.4 %copy-start.7 = (f32[1024]{0:T(1024)S(1)}, f32[1024]{0:T(1024)}, u32[]{:S(2)}) copy-start(f32[1024]{0:T(1024)} %copy-done.6) | copy-start | bytes 12292
Sparse Core Ops, SparseCore 0:
  115.9 110.1 reduce-scatter.6
  524.1 109.4 reduce-scatter.8
Sparse Core Ops, SparseCore 1:
  126.2 254.0 all-reduce.20
  520.3 253.3 all-reduce.22
where the time goes:
time: 834 us; the launch traced here: 819 us
  waiting for transfers between devices  501 us (60%)
  local copies, waits for them, and re-layouts  126 us (15%)
  blocking collectives  84.4 us (10%)
  matrix products  48.1 us (6%)
  other arithmetic  34.5 us (4%)
  between operations  16.4 us (2%)
  starting transfers between devices  8.87 us (1%)
    psum x2, waiting for transfers between devices, shards(): rel_total = lax.psum(rel_part, ('group', 'shard'))  393 us
    unnamed x6, waiting for transfers between devices  98.6 us
    all_gather x2, blocking collectives, shards(): negset = lax.all_gather(own_negative, 'shard', axis=0, tiled=True)  84.4 us
    another operation x22, local copies, waits for them, and re-layouts, local_pass(): jnp.stack([picture[row_off:row_off + height, col_off:col_off + across] fo...  27.5 us
  transfers between devices with their start and end apart: 8, of which 4 were waited for; matrix products, arithmetic and copies ran while one was open for 13% of the time, Pallas kernels for 0%

commit v1 on v0

v1 whole, which is shorter than its diff:
```python
import functools

import jax
import jax.numpy as jnp
import numpy as np
from jax import lax
from jax.experimental import pallas as pl
from jax.experimental.pallas import tpu as pltpu
from jax.sharding import PartitionSpec as P

D = 200
FILTERS = 32
FLAT = 10368
REL = 1387
REL_PAD = 1536
BLK = 48
TRI = 128
NEG = 32
ENT = 1024
CHUNK = 1152
STEPS = FLAT // CHUNK
MESH = pl.DeviceIdType.MESH
F32 = jnp.float32
BF16 = jnp.bfloat16

negative_weight = 0.03125
learn_rate = 0.5

NT = (((1,), (1,)), ((), ()))


def nn(a, b):
    return jnp.dot(a, b, preferred_element_type=F32)


def nt(a, b):
    return lax.dot_general(a, b, NT, preferred_element_type=F32)


def spread_dot(one_hot, values):
    high = values.astype(BF16)
    low = (values - high.astype(F32)).astype(BF16)
    return nn(one_hot, high) + nn(one_hot, low)


def hot_cols(ids_col, extent):
    where = lax.broadcasted_iota(jnp.int32, (ids_col.shape[0], extent), 1)
    return jnp.where(where == ids_col, 1.0, 0.0).astype(BF16)


def hot_rows(ids_row, extent):
    where = lax.broadcasted_iota(jnp.int32, (extent, ids_row.shape[1]), 0)
    return jnp.where(where == ids_row, 1.0, 0.0).astype(BF16)


def toeplitz_kernel(place_ref, wb_ref, t_ref, bias_ref):
    base = place_ref[0:1, :]
    filt = place_ref[1:2, :]
    own = jnp.where(
        lax.broadcasted_iota(jnp.int32, (FILTERS, CHUNK), 0) == filt, 1.0, 0.0
    ).astype(F32)
    wide = jnp.dot(wb_ref[...], own, precision=lax.Precision.HIGHEST, preferred_element_type=F32)
    bias_ref[...] = wide[9:10, :]
    for half in range(2):

        def tile(step, carry):
            first = pl.multiple_of(step * 16, 16)
            apart = lax.broadcasted_iota(jnp.int32, (16, CHUNK), 0) + (first + 200 * half) - base
            out = jnp.zeros((16, CHUNK), F32)
            for k in range(9):
                a, c = divmod(k, 3)
                out = jnp.where(apart == a * 20 + c, wide[k : k + 1, :], out)
            t_ref[half, pl.ds(first, 16), :] = out.astype(BF16)
            return carry

        lax.fori_loop(0, 13, tile, 0)


def toeplitz(conv_weight, conv_bias):
    q = np.arange(FLAT)
    rest = q % 324
    place = np.zeros((8, FLAT), np.int32)
    place[0] = (rest // 18) * 20 + rest % 18
    place[1] = q // 324
    wb = jnp.concatenate(
        [
            conv_weight.reshape(FILTERS, 9).astype(F32),
            conv_bias[:, None],
            jnp.zeros((FILTERS, 6), F32),
        ],
        axis=1,
    ).T
    return pl.pallas_call(
        toeplitz_kernel,
        grid=(STEPS,),
        out_shape=(
            jax.ShapeDtypeStruct((2, 208, FLAT), BF16),
            jax.ShapeDtypeStruct((1, FLAT), F32),
        ),
        in_specs=[
            pl.BlockSpec((8, CHUNK), lambda j: (0, j)),
            pl.BlockSpec((16, FILTERS), lambda j: (0, 0)),
        ],
        out_specs=(
            pl.BlockSpec((2, 208, CHUNK), lambda j: (0, 0, j)),
            pl.BlockSpec((1, CHUNK), lambda j: (0, j)),
        ),
        name="toeplitz",
    )(jnp.asarray(place), wb)


def pass_kernel(
    cols_ref, rows_ref, ent_ref, rel_ref, t_ref, w_ref, bias_ref, fc_bias_ref, tail_ref, neg_ref,
    head_out, rel_out, neg_out, tail_out,
    pic_h, pic_r, slope, acc, grad_h, grad_r, pre2_grad,
):
    phase = pl.program_id(0)
    step = pl.program_id(1)

    @pl.when((phase == 0) & (step == 0))
    def _():
        pic_h[...] = nn(hot_cols(cols_ref[:, 0:1], ENT), ent_ref[...].astype(BF16)).astype(BF16)
        pic_r[...] = nn(hot_cols(cols_ref[:, 1:2], REL), rel_ref[...].astype(BF16)).astype(BF16)
        acc[...] = jnp.zeros_like(acc)
        grad_h[...] = jnp.zeros_like(grad_h)
        grad_r[...] = jnp.zeros_like(grad_r)

    @pl.when(phase == 0)
    def _():
        pre1 = (
            nn(pic_h[...], t_ref[0, :D, :]) + nn(pic_r[...], t_ref[1, :D, :]) + bias_ref[...]
        )
        sigma = 0.5 * jnp.tanh(0.5 * pre1) + 0.5
        act = pre1 * sigma
        slope[step] = sigma + act * (1.0 - sigma)
        acc[...] += nn(act.astype(BF16), w_ref[...])

    @pl.when((phase == 0) & (step == STEPS - 1))
    def _():
        pre2 = acc[...] + fc_bias_ref[...]
        sigma = jax.nn.sigmoid(pre2)
        query = (pre2 * sigma).astype(BF16)
        tails = tail_ref[...].astype(F32)
        wide = query.astype(F32)
        pos_grad = -jax.nn.sigmoid(-jnp.sum(wide * tails, axis=1, keepdims=True))
        negset = neg_ref[...]
        by_row = (negative_weight * jax.nn.sigmoid(nt(query, negset))).astype(BF16)
        by_neg = (negative_weight * jax.nn.sigmoid(nt(negset, query))).astype(BF16)
        query_grad = pos_grad * tails + nn(by_row, negset)
        pre2_grad[...] = (query_grad * (sigma * (1.0 + pre2 * (1.0 - sigma)))).astype(BF16)
        neg_out[...] = nn(by_neg, query)
        tail_out[...] = pos_grad * wide

    @pl.when(phase == 1)
    def _():
        act_grad = nt(pre2_grad[...], w_ref[...])
        pre1_grad = (act_grad * slope[step]).astype(BF16)
        grad_h[...] += nt(pre1_grad, t_ref[0, :D, :])
        grad_r[...] += nt(pre1_grad, t_ref[1, :D, :])

    @pl.when((phase == 1) & (step == STEPS - 1))
    def _():
        head_out[...] = spread_dot(hot_rows(rows_ref[0:1, :], ENT), grad_h[...])
        rel_out[...] = spread_dot(hot_rows(rows_ref[1:2, :], REL_PAD), grad_r[...])


def block_pass(cols, rows, ent, rel, t_mat, fc_weight, bias, fc_bias, tails, negset):
    whole = lambda *shape: pl.BlockSpec(shape, lambda p, j: (0,) * len(shape))
    return pl.pallas_call(
        pass_kernel,
        grid=(2, STEPS),
        out_shape=(
            jax.ShapeDtypeStruct((ENT, D), F32),
            jax.ShapeDtypeStruct((REL_PAD, D), F32),
            jax.ShapeDtypeStruct((1024, D), F32),
            jax.ShapeDtypeStruct((TRI, D), F32),
        ),
        in_specs=[
            whole(TRI, 2),
            whole(2, TRI),
            whole(ENT, D),
            whole(REL, D),
            pl.BlockSpec((2, 208, CHUNK), lambda p, j: (0, 0, j)),
            pl.BlockSpec((CHUNK, D), lambda p, j: (j, 0)),
            pl.BlockSpec((1, CHUNK), lambda p, j: (0, j)),
            whole(1, D),
            whole(TRI, D),
            whole(1024, D),
        ],
        out_specs=(whole(ENT, D), whole(REL_PAD, D), whole(1024, D), whole(TRI, D)),
        scratch_shapes=[
            pltpu.VMEM((TRI, D), BF16),
            pltpu.VMEM((TRI, D), BF16),
            pltpu.VMEM((STEPS, TRI, CHUNK), F32),
            pltpu.VMEM((TRI, D), F32),
            pltpu.VMEM((TRI, D), F32),
            pltpu.VMEM((TRI, D), F32),
            pltpu.VMEM((TRI, D), BF16),
        ],
        compiler_params=pltpu.CompilerParams(vmem_limit_bytes=56 << 20),
        name="block_pass",
    )(cols, rows, ent, rel, t_mat, fc_weight, bias, fc_bias, tails, negset)


class Place:
    def __init__(self):
        group = lax.axis_index("group")
        shard = lax.axis_index("shard")
        self.x = group % 4
        self.y_hi = group // 4
        self.y_lo = shard // 16
        self.z = (shard // 2) % 8
        self.core = shard % 2
        self.y = self.y_hi * 2 + self.y_lo

    def at(self, x=None, y=None, z=None, core=None):
        x = self.x if x is None else x
        y = self.y if y is None else y
        z = self.z if z is None else z
        core = self.core if core is None else core
        return ((y // 2) * 4 + x, (y % 2) * 16 + z * 2 + core)

    def mate(self):
        return self.at(core=1 - self.core)

    def beside(self):
        return self.at(y=self.y_hi * 2 + 1 - self.y_lo)

    def partner(self, bit):
        if bit == 0:
            return self.at(x=self.x + 1 - 2 * (self.x % 2))
        return self.at(x=(self.x + 2) % 4)


class Copies:
    def __init__(self, send, recv):
        self.send, self.recv, self.used = send, recv, 0

    def start(self, src, dst, device):
        copy = pltpu.make_async_remote_copy(
            src_ref=src,
            dst_ref=dst,
            send_sem=self.send.at[self.used],
            recv_sem=self.recv.at[self.used],
            device_id=device,
            device_id_type=MESH,
        )
        self.used += 1
        copy.start()
        return copy


def greet(peers):
    barrier = pltpu.get_barrier_semaphore()
    for peer in peers:
        pl.semaphore_signal(barrier, inc=1, device_id=peer, device_id_type=MESH)
    pl.semaphore_wait(barrier, len(peers))


def wait_all(copies):
    for copy in copies:
        copy.wait()


def pick_rows(cols_ref, table_bf, pick_tail, pick_neg):
    pick_tail[...] = nn(hot_cols(cols_ref[0:TRI, :], ENT), table_bf).astype(BF16)
    pick_neg[...] = nn(hot_cols(cols_ref[TRI : TRI + NEG, :], ENT), table_bf).astype(BF16)


def rows_kernel(bit, cols_ref, ent_ref, tail_out, neg_out, pick_tail, pick_neg, tails, negs, send, recv):
    me = Place()
    copies = Copies(send, recv)
    pick_rows(cols_ref, ent_ref[...].astype(BF16), pick_tail, pick_neg)
    z_peers = [me.at(z=(me.z + d) % 8) for d in range(1, 8)]
    greet([me.mate(), me.beside(), me.partner(bit)] + z_peers)
    own = negs.at[me.core, me.y_lo, me.z]
    first = copies.start(pick_neg, own, me.partner(bit))
    tail = copies.start(pick_tail, tails, me.partner(bit))
    first.wait()
    wait_all([copies.start(own, own, peer) for peer in z_peers])
    half = negs.at[me.core, me.y_lo]
    copies.start(half, half, me.beside()).wait()
    half = negs.at[me.core]
    copies.start(half, half, me.mate()).wait()
    tail.wait()
    tail_out[...] = tails[...]
    neg_out[...] = negs[...]


VMEM_SPEC = pl.BlockSpec(memory_space=pltpu.VMEM)


def fetch_rows(bit, cols, ent):
    number = 11
    return pl.pallas_call(
        functools.partial(rows_kernel, bit),
        out_shape=(
            jax.ShapeDtypeStruct((TRI, D), BF16),
            jax.ShapeDtypeStruct((2, 2, 8, NEG, D), BF16),
        ),
        in_specs=[VMEM_SPEC] * 2,
        out_specs=(VMEM_SPEC, VMEM_SPEC),
        scratch_shapes=[
            pltpu.VMEM((TRI, D), BF16),
            pltpu.VMEM((NEG, D), BF16),
            pltpu.VMEM((TRI, D), BF16),
            pltpu.VMEM((2, 2, 8, NEG, D), BF16),
            pltpu.SemaphoreType.DMA((number,)),
            pltpu.SemaphoreType.DMA((number,)),
        ],
        compiler_params=pltpu.CompilerParams(collective_id=0, has_side_effects=True),
        name="fetch_rows",
    )(cols, ent)


def step_of(rows, state, gradient):
    state = state + jnp.sum(gradient * gradient, axis=1, keepdims=True) * (1.0 / D)
    return rows - learn_rate * gradient * lax.rsqrt(state), state


def update_kernel(
    bit, more,
    rel_part, neg_part, tail_grad, head_sum, ent, ent_state, rel, rel_state, rows_ref, *rest,
):
    if more:
        (cols_ref, ent_out, ent_state_out, rel_out, rel_state_out, tail_out, neg_out), rest = rest[:7], rest[7:]
    else:
        (ent_out, ent_state_out, rel_out, rel_state_out), rest = rest[:4], rest[4:]
    (r0, s1_send, s1_recv, acc1, s2_recv, z_buf, g_buf,
     b1, b2_send, b2_recv, b3_send, b3_recv, b4_send, b4_recv, tail_in), rest = rest[:15], rest[15:]
    if more:
        (pick_tail, pick_neg, tails, negs), rest = rest[:4], rest[4:]
    send, recv = rest
    me = Place()
    copies = Copies(send, recv)
    c, z, y_lo = me.core, me.z, me.y_lo
    first = me.x * (1 - c) + me.y * c
    second = me.y * (1 - c) + me.x * c

    def along_first(i):
        return me.at(x=i * (1 - c) + me.x * c, y=i * c + me.y * (1 - c))

    def along_second(i):
        return me.at(x=me.x * (1 - c) + i * c, y=i * (1 - c) + me.y * c)

    firsts = [(first + d) % 4 for d in range(1, 4)]
    seconds = [(second + d) % 4 for d in range(1, 4)]
    zs = [(z + d) % 8 for d in range(1, 8)]
    mate, partner = me.mate(), me.partner(bit)
    greet(
        [mate]
        + [along_first(i) for i in firsts]
        + [along_second(i) for i in seconds]
        + [me.at(z=i) for i in zs]
    )
    b1_copy = copies.start(neg_part.at[1 - c], b1, mate)
    s0_copy = copies.start(rel_part.at[1 - c], r0, mate)
    tail_copy = copies.start(tail_grad, tail_in, partner)
    b1_copy.wait()
    b2_send[...] = (neg_part[c, 1 - y_lo] + b1[1 - y_lo]).astype(BF16)
    b2_copy = copies.start(b2_send, b2_recv, me.beside())
    s0_copy.wait()
    for i in range(4):
        s1_send[i] = (rel_part[c, i] + r0[i]).astype(BF16)
    s1_copies = [
        copies.start(s1_send.at[i], s1_recv.at[d], along_first(i)) for d, i in enumerate(firsts)
    ]
    b2_copy.wait()
    b3_send[...] = (neg_part[c, y_lo] + b1[y_lo] + b2_recv[...].astype(F32)).astype(BF16)
    b3_copies = [
        copies.start(b3_send.at[i], b3_recv.at[d], me.at(z=i)) for d, i in enumerate(zs)
    ]
    wait_all(s1_copies)
    acc1[...] = (
        rel_part[c, first]
        + r0[first]
        + s1_recv[0].astype(F32)
        + s1_recv[1].astype(F32)
        + s1_recv[2].astype(F32)
    )
    s2_copies = [
        copies.start(acc1.at[i], s2_recv.at[d], along_second(i)) for d, i in enumerate(seconds)
    ]
    wait_all(s2_copies)
    z_buf[z] = (acc1[second] + s2_recv[0] + s2_recv[1] + s2_recv[2]).astype(BF16)
    z_copies = [copies.start(z_buf.at[z], z_buf.at[z], me.at(z=i)) for i in zs]
    wait_all(b3_copies)
    share = b3_send[z].astype(F32)
    for d in range(7):
        share = share + b3_recv[d].astype(F32)
    b4_send[...] = share
    b4_copy = copies.start(b4_send, b4_recv, partner)
    wait_all(z_copies)
    total = z_buf[0].astype(F32)
    for i in range(1, 8):
        total = total + z_buf[i].astype(F32)
    g_buf[c, first, second] = total.astype(BF16)
    own = g_buf.at[c, first, second]
    s4_copies = [copies.start(own, own, along_second(i)) for i in seconds]
    b4_copy.wait()
    tail_copy.wait()
    gradient = (
        head_sum[...]
        + spread_dot(hot_rows(rows_ref[0:1, 0:TRI], ENT), tail_in[...])
        + spread_dot(hot_rows(rows_ref[0:1, TRI : TRI + NEG], ENT), b4_recv[...])
    )
    new_rows, new_state = step_of(ent[...], ent_state[...], gradient)
    ent_out[...] = new_rows
    ent_state_out[...] = new_state
    if more:
        pick_rows(cols_ref, new_rows.astype(BF16), pick_tail, pick_neg)
        following = me.partner(1 - bit)
        mine = negs.at[c, y_lo, z]
        a1_copy = copies.start(pick_neg, mine, following)
        a0_copy = copies.start(pick_tail, tails, following)
    wait_all(s4_copies)
    own = g_buf.at[c, first]
    s5_copies = [copies.start(own, own, along_first(i)) for i in firsts]
    if more:
        a1_copy.wait()
        a2_copies = [copies.start(mine, mine, me.at(z=i)) for i in zs]
    wait_all(s5_copies)
    own = g_buf.at[c]
    s6_copy = copies.start(own, own, mate)
    if more:
        wait_all(a2_copies)
        half = negs.at[c, y_lo]
        a3_copy = copies.start(half, half, me.beside())
    s6_copy.wait()
    for k in range(29):
        low, high = k * BLK, min(k * BLK + BLK, REL)
        g = g_buf[k // 16, (k // 4) % 4, k % 4].astype(F32)[: high - low]
        new_rows, new_state = step_of(rel[low:high, :], rel_state[low:high, :], g)
        rel_out[low:high, :] = new_rows
        rel_state_out[low:high, :] = new_state
    if more:
        a3_copy.wait()
        half = negs.at[c]
        copies.start(half, half, mate).wait()
        a0_copy.wait()
        tail_out[...] = tails[...]
        neg_out[...] = negs[...]


def update(bit, more, rel_part, neg_part, tail_grad, head_sum, ent, ent_state, rel, rel_state, rows, cols):
    out_shape = [
        jax.ShapeDtypeStruct((ENT, D), F32),
        jax.ShapeDtypeStruct((ENT, 1), F32),
        jax.ShapeDtypeStruct((REL, D), F32),
        jax.ShapeDtypeStruct((REL, 1), F32),
    ]
    scratch = [
        pltpu.VMEM((4, 4, BLK, D), F32),
        pltpu.VMEM((4, 4, BLK, D), BF16),
        pltpu.VMEM((3, 4, BLK, D), BF16),
        pltpu.VMEM((4, BLK, D), F32),
        pltpu.VMEM((3, BLK, D), F32),
        pltpu.VMEM((8, BLK, D), BF16),
        pltpu.VMEM((2, 4, 4, BLK, D), BF16),
        pltpu.VMEM((2, 8, NEG, D), F32),
        pltpu.VMEM((8, NEG, D), BF16),
        pltpu.VMEM((8, NEG, D), BF16),
        pltpu.VMEM((8, NEG, D), BF16),
        pltpu.VMEM((7, NEG, D), BF16),
        pltpu.VMEM((NEG, D), F32),
        pltpu.VMEM((NEG, D), F32),
        pltpu.VMEM((TRI, D), F32),
    ]
    operands = [
        rel_part.reshape(2, 4, 4, BLK, D),
        neg_part.reshape(2, 2, 8, NEG, D),
        tail_grad, head_sum, ent, ent_state, rel, rel_state, rows,
    ]
    number = 1 + 1 + 1 + 1 + 3 + 7 + 3 + 7 + 1 + 3 + 3 + 1
    if more:
        number += 2 + 7 + 1 + 1
        operands.append(cols)
        out_shape += [
            jax.ShapeDtypeStruct((TRI, D), BF16),
            jax.ShapeDtypeStruct((2, 2, 8, NEG, D), BF16),
        ]
        scratch += [
            pltpu.VMEM((TRI, D), BF16),
            pltpu.VMEM((NEG, D), BF16),
            pltpu.VMEM((TRI, D), BF16),
            pltpu.VMEM((2, 2, 8, NEG, D), BF16),
        ]
    scratch += [pltpu.SemaphoreType.DMA((number,)), pltpu.SemaphoreType.DMA((number,))]
    return pl.pallas_call(
        functools.partial(update_kernel, bit, more),
        out_shape=tuple(out_shape),
        in_specs=[VMEM_SPEC] * len(operands),
        out_specs=tuple([VMEM_SPEC] * len(out_shape)),
        scratch_shapes=scratch,
        compiler_params=pltpu.CompilerParams(
            collective_id=1 + bit, has_side_effects=True, vmem_limit_bytes=56 << 20
        ),
        name="update",
    )(*operands)


def partner_ids(ids, bit):
    route = [(i, i ^ (1 << bit)) for i in range(8)]
    return lax.ppermute(ids, "group", route)


def shards(
    entity_rows, entity_state, relation_rows, relation_state,
    conv_weight, conv_bias, fc_weight, fc_bias,
    head_ids, rel_ids, tail_ids, neg_ids,
):
    asked = jnp.concatenate([tail_ids, neg_ids], axis=1)
    asked = [partner_ids(asked[r : r + 1], r) for r in range(2)]
    t_mat, bias = toeplitz(conv_weight, conv_bias)
    own_rows = [jnp.stack([head_ids[r], rel_ids[r]]) for r in range(2)]
    own_cols = [ids.T for ids in own_rows]
    asked_cols = [ids.reshape(TRI + NEG, 1) for ids in asked]
    ent, ent_state = entity_rows, entity_state.reshape(ENT, 1)
    rel, rel_state = relation_rows, relation_state.reshape(REL, 1)
    tails, negset = fetch_rows(0, asked_cols[0], ent)
    for r in range(2):
        head_sum, rel_part, neg_part, tail_grad = block_pass(
            own_cols[r], own_rows[r], ent, rel, t_mat, fc_weight, bias, fc_bias.reshape(1, D),
            tails, negset.reshape(1024, D),
        )
        out = update(
            r, r == 0, rel_part, neg_part, tail_grad, head_sum,
            ent, ent_state, rel, rel_state, asked[r], asked_cols[1],
        )
        ent, ent_state, rel, rel_state = out[:4]
        if r == 0:
            tails, negset = out[4:]
    return ent, ent_state.reshape(ENT), rel, rel_state.reshape(REL)


def solution(mesh):
    both = ("group", "shard")
    in_specs = (
        P(both, None), P(both), P(), P(), P(), P(), P(), P(),
        P(None, both), P(None, both), P(None, both), P(None, both),
    )
    out_specs = (P(both, None), P(both), P(), P())
    return jax.shard_map(shards, mesh=mesh, in_specs=in_specs, out_specs=out_specs, check_vma=False)
```

time: 834 us -> 210 us (0.25); the launches traced: 819 us -> 209 us
  waiting for transfers between devices: 501 us -> 0.01 us
  Pallas kernels: 0 us -> 178 us
  local copies, waits for them, and re-layouts: 126 us -> 22.8 us
  blocking collectives: 84.4 us -> 0 us
  matrix products: 48.1 us -> 0 us
  other arithmetic: 34.5 us -> 3.51 us
  between operations: 16.4 us -> 0.71 us
    psum x2 -> x0, waiting for transfers between devices: 393 us -> none  [shards(): rel_total = lax.psum(rel_part, ('group', 'shard'))]
    pallas_call x0 -> x6, Pallas kernels: none -> 178 us  [the longest x2 87.6 us: update(): pl.pallas_call(functools.partial(update_kernel, bit, more), out_shape=tup...]
    unnamed x6 -> x0, waiting for transfers between devices: 98.6 us -> none
    all_gather x2 -> x0, blocking collectives: 84.4 us -> none  [shards(): negset = lax.all_gather(own_negative, 'shard', axis=0, tiled=True)]
    dot_general x10 -> x0, matrix products: 44.6 us -> none  [the longest x2 11.8 us: local_pass(): jnp.einsum('fk,fijt->kijt', filters, pre1_grad, preferred_element_type=jn...]
    another operation x26 -> x0, local copies, waits for them, and re-layouts: 31.1 us -> none  [the longest x22 27.5 us: local_pass(): jnp.stack([picture[row_off:row_off + height, col_off:col_off + across] fo...]
    reshape x17 -> x4, local copies, waits for them, and re-layouts: 33.8 us -> 3.67 us  [the longest x2 1.53 us: shards(): asked_cols = [ids.reshape(TRI + NEG, 1) for ids in asked]]
    gather x14 -> x0, local copies, waits for them, and re-layouts: 18.8 us -> none  [the longest x4 6.17 us: shards(): ent_bf[heads]]
  transfers between devices with their start and end apart: 8 -> 2, of which waited for: 4 -> 0; matrix products, arithmetic and copies ran while one was open for 13% -> 9% of each run, Pallas kernels for 0% -> 9%
where the time goes in v1:
time: 210 us; the launch traced here: 209 us
  Pallas kernels  178 us (85%)
  local copies, waits for them, and re-layouts  22.8 us (11%)
  starting transfers between devices  4.48 us (2%)
  other arithmetic  3.51 us (2%)
    pallas_call x2, Pallas kernels, update(): pl.pallas_call(functools.partial(update_kernel, bit, more), out_shape=tup...  87.6 us
    pallas_call x2, Pallas kernels, block_pass(): pl.pallas_call(pass_kernel, grid=(2, STEPS), out_shape=(jax.ShapeDtypeStr...  49 us
    pallas_call x1, Pallas kernels, fetch_rows(): pl.pallas_call(functools.partial(rows_kernel, bit), out_shape=(jax.ShapeD...  23.2 us
    pallas_call x1, Pallas kernels, toeplitz(): pl.pallas_call(toeplitz_kernel, grid=(STEPS,), out_shape=(jax.ShapeDtypeS...  18 us
    unnamed x26, local copies, waits for them, and re-layouts  16.1 us
    ppermute x2, starting transfers between devices, partner_ids(): return lax.ppermute(ids, 'group', route)  4.48 us
  transfers between devices with their start and end apart: 2, of which 0 were waited for; matrix products, arithmetic and copies ran while one was open for 9% of the time, Pallas kernels for 9%

profile of v1, /device:TPU:1, one launch (start us, length us, event | category | flops | bytes accessed | tf_op | source)
XLA Modules:
  0.0 209.3 jit_solution(6788708865667963903)
XLA Ops:
  0.6 0.0 copy-start.8
  0.6 0.0 copy-start.9
  0.7 0.7 constant_dynamic-update-slice_fusion.1
  1.3 0.7 constant_dynamic-update-slice_fusion
  2.0 2.0 collective-permute-start
  4.1 2.5 %collective-permute-start.1 = (s32[1,160]{1,0:T(1,128)S(1)}, s32[1,160]{1,0:T(1,128)S(1)}, u32[]{:S(2)}, u32[]{:S(2)}) collective-permute-start(s32[1,160]{1,0:T(1,128)S(1)} %get-tuple-element.56), channel_id=1, source_target_pairs={{0,64},{32,96},{64,0},{96,32},{128,192},{160,224},{192,128},{224,1... | collective-permute-start | bytes 1928 | tf_op jit(solution)/shard_map/ppermute | solution.py:504
  6.5 0.8 fusion.3
  7.3 0.6 pad_add_fusion.1
  7.9 0.7 copy.30.cols_ref
  8.6 2.5 %copy.31.ent_ref.ent = f32[1024,200]{1,0:T(8,128)} copy(f32[1024,200]{0,1:T(8,128)} %param.13) | data formatting | bytes 1638400 | tf_op args[0]
  11.1 0.0 copy-done.8
  11.1 0.1 pad.2.clone
  11.2 0.6 pad_add_fusion
  11.7 0.0 copy-done.9
  11.7 0.7 maximum_bitcast_fusion.wb_ref
  12.4 0.0 copy-start
  12.4 7.4 %copy.33.w_ref = bf16[10368,200]{1,0:T(8,128)(2,1)} copy(bf16[10368,200]{0,1:T(8,128)(2,1)} %param.19) | data formatting | bytes 8294400 | tf_op args[6]
  19.8 0.0 copy-done
  19.8 0.0 copy-start.4
  19.8 0.0 copy-start.5
  19.8 1.5 copy.32.rel_ref.rel
  21.3 0.0 copy-done.4
  21.3 1.1 reshape.65.rel_state
  22.4 0.0 copy-done.5
  22.4 1.0 copy.35.ent_state
  23.5 0.7 copy.39.cols_ref
  24.2 18.0 %toeplitz.1 = (bf16[2,208,10368]{2,1,0:T(8,128)(2,1)}, f32[1,10368]{1,0:T(1,128)}) custom-call(s32[8,10368]{1,0:T(8,128)} %constant.4.clone.place_ref, f32[16,32]{1,0:T(8,128)} %maximum_bitcast_fusion.wb_ref), custom_call_target="tpu_custom_call" | custom-call | tf_op jit(solution)/shard_map/toeplitz/pallas_call | solution.py:93
  42.2 0.0 collective-permute-done.rows_ref
  42.2 0.0 copy-start.7
  42.2 0.8 copy.28.cols_ref
  43.0 0.0 collective-permute-done.1.rows_ref
  43.0 0.0 copy-start.6
  43.0 0.8 copy.38.rest_0_
  43.7 23.2 %fetch_rows.1 = (bf16[128,200]{1,0:T(8,128)(2,1)}, bf16[2,2,8,32,200]{4,3,2,1,0:T(8,128)(2,1)}) custom-call(s32[160,1]{1,0:T(8,128)} %copy.28.cols_ref, f32[1024,200]{1,0:T(8,128)} %copy.31.ent_ref.ent), custom_call_target="tpu_custom_call" | custom-call | tf_op jit(solution)/shard_map/fetch_rows/pallas_call | solution.py:295
  67.0 24.5 %block_pass.2 = (f32[1024,200]{1,0:T(8,128)}, f32[1536,200]{1,0:T(8,128)}, f32[1024,200]{1,0:T(8,128)}, f32[128,200]{1,0:T(8,128)}) custom-call(s32[128,2]{1,0:T(8,128)} %copy.30.cols_ref, s32[2,128]{1,0:T(2,128)} %get-tuple-element.58.rows_ref, f32[1024,200]{1,0:T(8,128)} %copy.31.ent_ref.ent, f32[1387,200]{1,0:T(8,128)} %copy.32.rel_ref.rel, ...), custom_call_target="tpu_custom_call" | custom-call | tf_op jit(solution)/shard_map/block_pass/pallas_call | solution.py:169
  91.5 0.0 copy-done.7
  91.5 0.0 copy-done.6
  91.5 47.1 %update.2 = (f32[1024,200]{1,0:T(8,128)}, f32[1024,1]{1,0:T(8,128)}, f32[1387,200]{1,0:T(8,128)}, f32[1387,1]{1,0:T(8,128)}, bf16[128,200]{1,0:T(8,128)(2,1)}, /*index=5*/bf16[2,2,8,32,200]{4,3,2,1,0:T(8,128)(2,1)}) custom-call(f32[2,4,4,48,200]{4,3,2,1,0:T(8,128)} %bitcast.20, f32[2,2,8,32,200]{4,3,2,1,0:T(8,128)} %bitcast.22, ...), custom_call_target="tpu_custom_call" | custom-call | tf_op jit(solution)/shard_map/update/pallas_call | solution.py:489
  138.6 24.5 %block_pass.3 = (f32[1024,200]{1,0:T(8,128)}, f32[1536,200]{1,0:T(8,128)}, f32[1024,200]{1,0:T(8,128)}, f32[128,200]{1,0:T(8,128)}) custom-call(s32[128,2]{1,0:T(8,128)} %copy.39.cols_ref, s32[2,128]{1,0:T(2,128)} %get-tuple-element.64.rows_ref, f32[1024,200]{1,0:T(8,128)} %get-tuple-element.34.ent_ref.ent, f32[1387,200]{1,0:T(8,128)} %get-tuple-element.35.rel_ref.rel, ...), custom_call_target="tpu_custom_call" | custom-call | tf_op jit(solution)/shard_map/block_pass/pallas_call | solution.py:169
  163.1 40.5 %update.3 = (f32[1024,200]{1,0:T(8,128)}, f32[1024,1]{1,0:T(8,128)}, f32[1387,200]{1,0:T(8,128)}, f32[1387,1]{1,0:T(8,128)}) custom-call(f32[2,4,4,48,200]{4,3,2,1,0:T(8,128)} %bitcast.19, f32[2,2,8,32,200]{4,3,2,1,0:T(8,128)} %bitcast.21, f32[128,200]{1,0:T(8,128)} %get-tuple-element.40.tail_grad, f32[1024,200]{1,0:T(8,128)} %get-tuple-element.41.head_sum, ...), custom_call_target="tpu_custom_call" | custom-call | tf_op jit(solution)/shard_map/update/pallas_call | solution.py:489
  203.5 0.0 copy-start.1
  203.6 2.9 %copy.42 = f32[1387,200]{0,1:T(8,128)} copy(f32[1387,200]{1,0:T(8,128)} %get-tuple-element.54) | data formatting | bytes 2219200
  206.4 0.0 copy-start.2
  206.4 0.0 copy-start.3
  206.4 0.0 copy-done.1
  206.4 1.2 copy.41
  207.6 0.0 copy-done.2
  207.6 0.9 reduce.1
  208.5 0.0 copy-done.3
  208.5 0.8 reduce
  (3 shorter events, 0.0 us)
Async XLA Ops:
  0.6 10.4 %copy-start.8 = (bf16[32,3,3]{0,2,1:T(4,128)(2,1)S(1)}, bf16[32,3,3]{0,2,1:T(4,128)(2,1)}, u32[]{:S(2)}) copy-start(bf16[32,3,3]{0,2,1:T(4,128)(2,1)} %param.17) | copy-start | bytes 1732
  0.6 11.1 %copy-start.9 = (f32[32]{0:T(128)S(1)}, f32[32]{0:T(128)}, u32[]{:S(2)}) copy-start(f32[32]{0:T(128)} %param.18) | copy-start | bytes 388
  2.0 40.2 %collective-permute-start = (s32[1,160]{1,0:T(1,128)S(1)}, s32[1,160]{1,0:T(1,128)S(1)}, u32[]{:S(2)}, u32[]{:S(2)}) collective-permute-start(s32[1,160]{1,0:T(1,128)S(1)} %get-tuple-element.57), channel_id=1, source_target_pairs={{0,32},{32,0},{64,96},{96,64},{128,160},{160,128},{192,224},{224,1... | collective-permute-start | bytes 1928 | tf_op jit(solution)/shard_map/ppermute | solution.py:504
  4.1 38.9 %collective-permute-start.1 = (s32[1,160]{1,0:T(1,128)S(1)}, s32[1,160]{1,0:T(1,128)S(1)}, u32[]{:S(2)}, u32[]{:S(2)}) collective-permute-start(s32[1,160]{1,0:T(1,128)S(1)} %get-tuple-element.56), channel_id=1, source_target_pairs={{0,64},{32,96},{64,0},{96,32},{128,192},{160,224},{192,128},{224,1... | collective-permute-start | bytes 1928 | tf_op jit(solution)/shard_map/ppermute | solution.py:504
  12.4 7.4 %copy-start = (f32[1387,200]{0,1:T(8,128)S(1)}, f32[1387,200]{0,1:T(8,128)}, u32[]{:S(2)}) copy-start(f32[1387,200]{0,1:T(8,128)} %param.15) | copy-start | bytes 3328804
  19.8 1.5 copy-start.4
  19.8 2.6 %copy-start.5 = (f32[1024]{0:T(1024)S(1)}, f32[1024]{0:T(1024)}, u32[]{:S(2)}) copy-start(f32[1024]{0:T(1024)} %param.14) | copy-start | bytes 12292
  42.2 49.3 %copy-start.7 = (s32[1,160]{1,0:T(1,128)}, s32[1,160]{1,0:T(1,128)S(1)}, u32[]{:S(2)}) copy-start(s32[1,160]{1,0:T(1,128)S(1)} %collective-permute-done.rows_ref) | copy-start | bytes 1924
  43.0 48.5 %copy-start.6 = (s32[1,160]{1,0:T(1,128)}, s32[1,160]{1,0:T(1,128)S(1)}, u32[]{:S(2)}) copy-start(s32[1,160]{1,0:T(1,128)S(1)} %collective-permute-done.1.rows_ref) | copy-start | bytes 1924
  203.5 2.9 %copy-start.1 = (f32[1024,200]{1,0:T(8,128)S(1)}, f32[1024,200]{1,0:T(8,128)}, u32[]{:S(2)}) copy-start(f32[1024,200]{1,0:T(8,128)} %get-tuple-element.52) | copy-start | bytes 2457604
  206.4 1.2 copy-start.2
  206.4 2.1 %copy-start.3 = (f32[1024,1]{1,0:T(8,128)S(1)}, f32[1024,1]{1,0:T(8,128)}, u32[]{:S(2)}) copy-start(f32[1024,1]{1,0:T(8,128)} %get-tuple-element.45) | copy-start | bytes 12292

commit v2 on v1

v2 whole, which is shorter than its diff:
```python
import functools

import jax
import jax.numpy as jnp
import numpy as np
from jax import lax
from jax.experimental import pallas as pl
from jax.experimental.pallas import tpu as pltpu
from jax.sharding import PartitionSpec as P

D = 200
FILTERS = 32
FLAT = 10368
REL = 1387
REL_PAD = 1536
BLK = 48
TRI = 128
NEG = 32
ENT = 1024
CHUNK = 1152
STEPS = FLAT // CHUNK
WIDE = 240
MESH = pl.DeviceIdType.MESH
F32 = jnp.float32
BF16 = jnp.bfloat16

negative_weight = 0.03125
learn_rate = 0.5

NT = (((1,), (1,)), ((), ()))


def nn(a, b):
    return jnp.dot(a, b, preferred_element_type=F32)


def nt(a, b):
    return lax.dot_general(a, b, NT, preferred_element_type=F32)


def spread_dot(one_hot, values):
    high = values.astype(BF16)
    low = (values - high.astype(F32)).astype(BF16)
    return nn(one_hot, high) + nn(one_hot, low)


def hot_rows(ids_row, extent):
    where = lax.broadcasted_iota(jnp.int32, (extent, ids_row.shape[1]), 0)
    return jnp.where(where == ids_row, 1.0, 0.0).astype(BF16)


def spacing():
    d = np.arange(D)
    out = np.zeros((D, WIDE), np.float32)
    out[d, d // 20 * 24 + d % 20] = 1.0
    return jnp.asarray(out, BF16)


def spread_nt(one_hot, values):
    high = values.astype(BF16)
    low = (values - high.astype(F32)).astype(BF16)
    return nt(one_hot, high) + nt(one_hot, low)


def spread_nt_right(values, one_hot):
    high = values.astype(BF16)
    low = (values - high.astype(F32)).astype(BF16)
    return nt(high, one_hot) + nt(low, one_hot)


def pass_kernel(
    round_index,
    head_ids, rel_ids, ent_ref, rel_ref, t_hbm, w_hbm, bias_ref, fc_bias_ref, tail_ref, neg_ref, space_ref,
    head_out, rel_out, neg_out, tail_out,
    t_all, w_all, pic_h, pic_r, slope, acc, grad_h, grad_r, pre2_grad, t_sem, w_sem,
):
    phase = pl.program_id(0)
    step = pl.program_id(1)

    def fetch(j):
        return (
            pltpu.make_async_copy(t_hbm.at[j], t_all.at[j], t_sem.at[j]),
            pltpu.make_async_copy(
                w_hbm.at[:, pl.ds(pl.multiple_of(j * CHUNK, CHUNK), CHUNK)], w_all.at[j], w_sem.at[j]
            ),
        )

    @pl.when((phase == 0) & (step == 0))
    def _():
        for j in range(STEPS):
            for copy in fetch(j):
                copy.start()
        heads = nn(ent_ref[...].astype(BF16), hot_rows(head_ids[round_index : round_index + 1, :], ENT))
        pic_h[...] = nn(heads.T.astype(BF16), space_ref[...]).astype(BF16)
        relations = nn(rel_ref[...].astype(BF16), hot_rows(rel_ids[round_index : round_index + 1, :], REL))
        pic_r[...] = nn(relations.T.astype(BF16), space_ref[...]).astype(BF16)
        acc[...] = jnp.zeros_like(acc)
        grad_h[...] = jnp.zeros_like(grad_h)
        grad_r[...] = jnp.zeros_like(grad_r)

    @pl.when(phase == 0)
    def _():
        for copy in fetch(step):
            copy.wait()
        pre1 = nn(pic_h[...], t_all[step, 0]) + nn(pic_r[...], t_all[step, 1]) + bias_ref[step]
        sigma = 0.5 * jnp.tanh(0.5 * pre1) + 0.5
        act = pre1 * sigma
        slope[step] = sigma + act * (1.0 - sigma)
        acc[...] += nt(act.astype(BF16), w_all[step])

    @pl.when((phase == 0) & (step == STEPS - 1))
    def _():
        pre2 = acc[...] + fc_bias_ref[...]
        sigma = jax.nn.sigmoid(pre2)
        query = (pre2 * sigma).astype(BF16)
        tails = tail_ref[...].astype(F32)
        wide = query.astype(F32)
        pos_grad = -jax.nn.sigmoid(-jnp.sum(wide * tails, axis=1, keepdims=True))
        negset = neg_ref[...]
        by_row = (negative_weight * jax.nn.sigmoid(nt(query, negset))).astype(BF16)
        by_neg = (negative_weight * jax.nn.sigmoid(nt(negset, query))).astype(BF16)
        query_grad = pos_grad * tails + nn(by_row, negset)
        pre2_grad[...] = (query_grad * (sigma * (1.0 + pre2 * (1.0 - sigma)))).astype(BF16)
        neg_out[...] = nn(by_neg, query).astype(BF16)
        tail_out[...] = (pos_grad * wide).T

    @pl.when(phase == 1)
    def _():
        act_grad = nn(pre2_grad[...], w_all[step])
        pre1_grad = (act_grad * slope[step]).astype(BF16)
        grad_h[...] += nt(pre1_grad, t_all[step, 0])
        grad_r[...] += nt(pre1_grad, t_all[step, 1])

    @pl.when((phase == 1) & (step == STEPS - 1))
    def _():
        head_out[...] = spread_nt(space_ref[...], grad_h[...])
        rows = spread_nt_right(grad_r[...], space_ref[...])
        rel_out[...] = spread_dot(hot_rows(rel_ids[round_index : round_index + 1, :], REL_PAD), rows).astype(BF16)


def block_pass(round_index, head_ids, rel_ids, ent, rel, t_mat, w_mat, bias, fc_bias, tails, negset):
    whole = lambda *shape: pl.BlockSpec(shape, lambda p, j: (0,) * len(shape))
    anywhere = pl.BlockSpec(memory_space=pl.ANY)
    return pl.pallas_call(
        functools.partial(pass_kernel, round_index),
        grid=(2, STEPS),
        out_shape=(
            jax.ShapeDtypeStruct((D, TRI), F32),
            jax.ShapeDtypeStruct((REL_PAD, D), BF16),
            jax.ShapeDtypeStruct((1024, D), BF16),
            jax.ShapeDtypeStruct((D, TRI), F32),
        ),
        in_specs=[
            whole(2, TRI),
            whole(2, TRI),
            whole(D, ENT),
            whole(D, REL),
            anywhere,
            anywhere,
            whole(STEPS, 1, CHUNK),
            whole(1, D),
            whole(TRI, D),
            whole(1024, D),
            whole(D, WIDE),
        ],
        out_specs=(whole(D, TRI), whole(REL_PAD, D), whole(1024, D), whole(D, TRI)),
        scratch_shapes=[
            pltpu.VMEM((STEPS, 2, WIDE, CHUNK), BF16),
            pltpu.VMEM((STEPS, D, CHUNK), BF16),
            pltpu.VMEM((TRI, WIDE), BF16),
            pltpu.VMEM((TRI, WIDE), BF16),
            pltpu.VMEM((STEPS, TRI, CHUNK), F32),
            pltpu.VMEM((TRI, D), F32),
            pltpu.VMEM((TRI, WIDE), F32),
            pltpu.VMEM((TRI, WIDE), F32),
            pltpu.VMEM((TRI, D), BF16),
            pltpu.SemaphoreType.DMA((STEPS,)),
            pltpu.SemaphoreType.DMA((STEPS,)),
        ],
        compiler_params=pltpu.CompilerParams(vmem_limit_bytes=56 << 20),
        name="block_pass",
    )(head_ids, rel_ids, ent, rel, t_mat, w_mat, bias, fc_bias, tails, negset, spacing())


class Place:
    def __init__(self):
        group = lax.axis_index("group")
        shard = lax.axis_index("shard")
        self.x = group % 4
        self.y_hi = group // 4
        self.y_lo = shard // 16
        self.z = (shard // 2) % 8
        self.core = shard % 2
        self.y = self.y_hi * 2 + self.y_lo

    def at(self, x=None, y=None, z=None, core=None):
        x = self.x if x is None else x
        y = self.y if y is None else y
        z = self.z if z is None else z
        core = self.core if core is None else core
        return ((y // 2) * 4 + x, (y % 2) * 16 + z * 2 + core)

    def mate(self):
        return self.at(core=1 - self.core)

    def beside(self):
        return self.at(y=self.y_hi * 2 + 1 - self.y_lo)

    def partner(self, bit):
        if bit == 0:
            return self.at(x=self.x + 1 - 2 * (self.x % 2))
        return self.at(x=(self.x + 2) % 4)


class Copies:
    def __init__(self, send, recv):
        self.send, self.recv, self.used = send, recv, 0

    def start(self, src, dst, device):
        copy = pltpu.make_async_remote_copy(
            src_ref=src,
            dst_ref=dst,
            send_sem=self.send.at[self.used],
            recv_sem=self.recv.at[self.used],
            device_id=device,
            device_id_type=MESH,
        )
        self.used += 1
        copy.start()
        return copy


def greet(peers):
    barrier = pltpu.get_barrier_semaphore()
    for peer in peers:
        pl.semaphore_signal(barrier, inc=1, device_id=peer, device_id_type=MESH)
    pl.semaphore_wait(barrier, len(peers))


def wait_all(copies):
    for copy in copies:
        copy.wait()


def pick_rows(tail_ids, neg_ids, table_bf, pick_tail, pick_neg):
    pick_tail[...] = nn(table_bf, hot_rows(tail_ids, ENT)).T.astype(BF16)
    pick_neg[...] = nn(table_bf, hot_rows(neg_ids, ENT)).T.astype(BF16)


def toeplitz_chunk(j, place_ref, wb_ref, columns, t_all, bias_out):
    lanes = slice(j * CHUNK, (j + 1) * CHUNK)
    down, across, filt = (place_ref[k : k + 1, lanes] for k in range(3))
    own = jnp.where(
        lax.broadcasted_iota(jnp.int32, (FILTERS, CHUNK), 0) == filt, 1.0, 0.0
    ).astype(F32)
    wide = jnp.dot(wb_ref[...], own, precision=lax.Precision.HIGHEST, preferred_element_type=F32)
    bias_out[j] = wide[9:10, :]
    apart = lax.broadcasted_iota(jnp.int32, (24, CHUNK), 0) - across
    for a in range(3):
        out = jnp.zeros((24, CHUNK), F32)
        for c in range(3):
            out = jnp.where(apart == c, wide[3 * a + c : 3 * a + c + 1, :], out)
        columns[a] = out
    for half in range(2):

        def pair(p, carry):
            rows = []
            for one in range(2):
                away = (10 * half + 2 * p + one) - down
                out = jnp.where(away == 2, columns[2], 0.0)
                out = jnp.where(away == 1, columns[1], out)
                rows.append(jnp.where(away == 0, columns[0], out))
            first = pl.multiple_of(p * 48, 48)
            t_all[j, half, pl.ds(first, 48), :] = jnp.concatenate(rows, axis=0).astype(BF16)
            return carry

        lax.fori_loop(0, 5, pair, 0)


def rows_kernel(
    tail_ids, neg_ids, ent_ref, place_ref, wb_ref,
    tail_out, neg_out, t_out, bias_out, asked_tail, asked_neg,
    tails_in, negs_in, pick_tail, pick_neg, tails, negs, columns, t_all, t_sem, send, recv,
):
    me = Place()
    copies = Copies(send, recv)
    z_peers = [me.at(z=(me.z + d) % 8) for d in range(1, 8)]
    partners = [me.partner(0), me.partner(1)]
    greet([me.mate(), me.beside()] + partners + z_peers)
    asked = [
        (copies.start(tail_ids, tails_in.at[r], partners[r]), copies.start(neg_ids, negs_in.at[r], partners[r]))
        for r in range(2)
    ]
    out_copies = []

    def build(j):
        toeplitz_chunk(j, place_ref, wb_ref, columns, t_all, bias_out)
        copy = pltpu.make_async_copy(t_all.at[j], t_out.at[j], t_sem.at[j])
        copy.start()
        out_copies.append(copy)

    build(0)
    build(1)
    wait_all(asked[0])
    wait_all(asked[1])
    for r in range(2):
        asked_tail[r : r + 1, :] = tails_in[r, r : r + 1, :]
        asked_neg[r : r + 1, :] = negs_in[r, r : r + 1, :]
    pick_rows(tails_in[0, 0:1, :], negs_in[0, 0:1, :], ent_ref[...].astype(BF16), pick_tail, pick_neg)
    own = negs.at[me.core, me.y_lo, me.z]
    first = copies.start(pick_neg, own, partners[0])
    tail = copies.start(pick_tail, tails, partners[0])
    build(2)
    build(3)
    first.wait()
    z_copies = [copies.start(own, own, peer) for peer in z_peers]
    for j in range(4, 7):
        build(j)
    wait_all(z_copies)
    half = negs.at[me.core, me.y_lo]
    copy = copies.start(half, half, me.beside())
    for j in range(7, STEPS):
        build(j)
    copy.wait()
    half = negs.at[me.core]
    copies.start(half, half, me.mate()).wait()
    tail.wait()
    tail_out[...] = tails[...]
    neg_out[...] = negs[...]
    wait_all(out_copies)


VMEM_SPEC = pl.BlockSpec(memory_space=pltpu.VMEM)


def fetch_rows(tail_ids, neg_ids, ent, conv_weight, conv_bias):
    number = 15
    q = np.arange(FLAT)
    place = np.zeros((8, FLAT), np.int32)
    place[0] = q % 324 // 18
    place[1] = q % 18
    place[2] = q // 324
    wb = jnp.concatenate(
        [conv_weight.reshape(FILTERS, 9).astype(F32), conv_bias[:, None], jnp.zeros((FILTERS, 6), F32)],
        axis=1,
    ).T
    return pl.pallas_call(
        rows_kernel,
        out_shape=(
            jax.ShapeDtypeStruct((TRI, D), BF16),
            jax.ShapeDtypeStruct((2, 2, 8, NEG, D), BF16),
            jax.ShapeDtypeStruct((STEPS, 2, WIDE, CHUNK), BF16),
            jax.ShapeDtypeStruct((STEPS, 1, CHUNK), F32),
            jax.ShapeDtypeStruct((2, TRI), jnp.int32),
            jax.ShapeDtypeStruct((2, NEG), jnp.int32),
        ),
        in_specs=[VMEM_SPEC] * 5,
        out_specs=(
            VMEM_SPEC, VMEM_SPEC, pl.BlockSpec(memory_space=pl.ANY), VMEM_SPEC, VMEM_SPEC, VMEM_SPEC,
        ),
        scratch_shapes=[
            pltpu.VMEM((2, 2, TRI), jnp.int32),
            pltpu.VMEM((2, 2, NEG), jnp.int32),
            pltpu.VMEM((TRI, D), BF16),
            pltpu.VMEM((NEG, D), BF16),
            pltpu.VMEM((TRI, D), BF16),
            pltpu.VMEM((2, 2, 8, NEG, D), BF16),
            pltpu.VMEM((3, 24, CHUNK), F32),
            pltpu.VMEM((STEPS, 2, WIDE, CHUNK), BF16),
            pltpu.SemaphoreType.DMA((STEPS,)),
            pltpu.SemaphoreType.DMA((number,)),
            pltpu.SemaphoreType.DMA((number,)),
        ],
        compiler_params=pltpu.CompilerParams(
            collective_id=0, has_side_effects=True, vmem_limit_bytes=40 << 20
        ),
        name="fetch_rows",
    )(tail_ids, neg_ids, ent, jnp.asarray(place), wb)


def step_of(rows, state, gradient):
    state = state + jnp.sum(gradient * gradient, axis=0, keepdims=True) * (1.0 / D)
    return rows - learn_rate * gradient * lax.rsqrt(state), state


def update_kernel(
    bit, more,
    rel_part, neg_part, tail_grad, head_grad, ent, ent_state, rel, rel_state, head_ids, asked_tail, asked_neg,
    *rest,
):
    if more:
        (ent_out, ent_state_out, rel_out, rel_state_out, tail_out, neg_out), rest = rest[:6], rest[6:]
    else:
        (ent_out, ent_state_out, rel_out, rel_state_out), rest = rest[:4], rest[4:]
    (r0, s1_send, s1_recv, acc1, s2_recv, z_buf, g_buf,
     b1, b2_send, b2_recv, b3_send, b3_recv, b4_send, b4_recv, tail_in), rest = rest[:15], rest[15:]
    if more:
        (pick_tail, pick_neg, tails, negs), rest = rest[:4], rest[4:]
    send, recv = rest
    me = Place()
    copies = Copies(send, recv)
    c, z, y_lo = me.core, me.z, me.y_lo
    first = me.x * (1 - c) + me.y * c
    second = me.y * (1 - c) + me.x * c

    def along_first(i):
        return me.at(x=i * (1 - c) + me.x * c, y=i * c + me.y * (1 - c))

    def along_second(i):
        return me.at(x=me.x * (1 - c) + i * c, y=i * (1 - c) + me.y * c)

    firsts = [(first + d) % 4 for d in range(1, 4)]
    seconds = [(second + d) % 4 for d in range(1, 4)]
    zs = [(z + d) % 8 for d in range(1, 8)]
    mate, partner = me.mate(), me.partner(bit)
    greet(
        [mate]
        + [along_first(i) for i in firsts]
        + [along_second(i) for i in seconds]
        + [me.at(z=i) for i in zs]
    )
    b1_copy = copies.start(neg_part.at[1 - c], b1, mate)
    s0_copy = copies.start(rel_part.at[1 - c], r0, mate)
    tail_copy = copies.start(tail_grad, tail_in, partner)
    b1_copy.wait()
    b2_send[...] = (neg_part[c, 1 - y_lo].astype(F32) + b1[1 - y_lo].astype(F32)).astype(BF16)
    b2_copy = copies.start(b2_send, b2_recv, me.beside())
    s0_copy.wait()
    for i in range(4):
        s1_send[i] = (rel_part[c, i].astype(F32) + r0[i].astype(F32)).astype(BF16)
    s1_copies = [
        copies.start(s1_send.at[i], s1_recv.at[d], along_first(i)) for d, i in enumerate(firsts)
    ]
    b2_copy.wait()
    b3_send[...] = (
        neg_part[c, y_lo].astype(F32) + b1[y_lo].astype(F32) + b2_recv[...].astype(F32)
    ).astype(BF16)
    b3_copies = [
        copies.start(b3_send.at[i], b3_recv.at[d], me.at(z=i)) for d, i in enumerate(zs)
    ]
    wait_all(s1_copies)
    acc1[...] = (
        rel_part[c, first].astype(F32)
        + r0[first].astype(F32)
        + s1_recv[0].astype(F32)
        + s1_recv[1].astype(F32)
        + s1_recv[2].astype(F32)
    )
    s2_copies = [
        copies.start(acc1.at[i], s2_recv.at[d], along_second(i)) for d, i in enumerate(seconds)
    ]
    wait_all(s2_copies)
    z_buf[z] = (acc1[second] + s2_recv[0] + s2_recv[1] + s2_recv[2]).astype(BF16)
    z_copies = [copies.start(z_buf.at[z], z_buf.at[z], me.at(z=i)) for i in zs]
    wait_all(b3_copies)
    share = b3_send[z].astype(F32)
    for d in range(7):
        share = share + b3_recv[d].astype(F32)
    b4_send[...] = share
    b4_copy = copies.start(b4_send, b4_recv, partner)
    wait_all(z_copies)
    total = z_buf[0].astype(F32)
    for i in range(1, 8):
        total = total + z_buf[i].astype(F32)
    g_buf[c, first, second] = total.astype(BF16)
    own = g_buf.at[c, first, second]
    s4_copies = [copies.start(own, own, along_second(i)) for i in seconds]
    b4_copy.wait()
    tail_copy.wait()
    gradient = (
        spread_nt_right(head_grad[...], hot_rows(head_ids[bit : bit + 1, :], ENT))
        + spread_nt_right(tail_in[...], hot_rows(asked_tail[bit : bit + 1, :], ENT))
        + spread_nt_right(b4_recv[...].T, hot_rows(asked_neg[bit : bit + 1, :], ENT))
    )
    new_rows, new_state = step_of(ent[...], ent_state[...], gradient)
    ent_out[...] = new_rows
    ent_state_out[...] = new_state
    if more:
        pick_rows(asked_tail[1:2, :], asked_neg[1:2, :], new_rows.astype(BF16), pick_tail, pick_neg)
        following = me.partner(1 - bit)
        mine = negs.at[c, y_lo, z]
        a1_copy = copies.start(pick_neg, mine, following)
        a0_copy = copies.start(pick_tail, tails, following)
    wait_all(s4_copies)
    own = g_buf.at[c, first]
    s5_copies = [copies.start(own, own, along_first(i)) for i in firsts]
    if more:
        a1_copy.wait()
        a2_copies = [copies.start(mine, mine, me.at(z=i)) for i in zs]
    wait_all(s5_copies)
    own = g_buf.at[c]
    s6_copy = copies.start(own, own, mate)
    if more:
        wait_all(a2_copies)
        half = negs.at[c, y_lo]
        a3_copy = copies.start(half, half, me.beside())
    s6_copy.wait()
    eye = jnp.where(
        lax.broadcasted_iota(jnp.int32, (D, D), 0) == lax.broadcasted_iota(jnp.int32, (D, D), 1), 1.0, 0.0
    ).astype(BF16)
    gradient = nt(eye, g_buf[...].reshape(REL_PAD, D))[:, :REL]
    new_rows, new_state = step_of(rel[...], rel_state[...], gradient)
    rel_out[...] = new_rows
    rel_state_out[...] = new_state
    if more:
        a3_copy.wait()
        half = negs.at[c]
        copies.start(half, half, mate).wait()
        a0_copy.wait()
        tail_out[...] = tails[...]
        neg_out[...] = negs[...]


def update(
    bit, more, rel_part, neg_part, tail_grad, head_grad, ent, ent_state, rel, rel_state,
    head_ids, asked_tail, asked_neg,
):
    out_shape = [
        jax.ShapeDtypeStruct((D, ENT), F32),
        jax.ShapeDtypeStruct((1, ENT), F32),
        jax.ShapeDtypeStruct((D, REL), F32),
        jax.ShapeDtypeStruct((1, REL), F32),
    ]
    scratch = [
        pltpu.VMEM((4, 4, BLK, D), BF16),
        pltpu.VMEM((4, 4, BLK, D), BF16),
        pltpu.VMEM((3, 4, BLK, D), BF16),
        pltpu.VMEM((4, BLK, D), F32),
        pltpu.VMEM((3, BLK, D), F32),
        pltpu.VMEM((8, BLK, D), BF16),
        pltpu.VMEM((2, 4, 4, BLK, D), BF16),
        pltpu.VMEM((2, 8, NEG, D), BF16),
        pltpu.VMEM((8, NEG, D), BF16),
        pltpu.VMEM((8, NEG, D), BF16),
        pltpu.VMEM((8, NEG, D), BF16),
        pltpu.VMEM((7, NEG, D), BF16),
        pltpu.VMEM((NEG, D), F32),
        pltpu.VMEM((NEG, D), F32),
        pltpu.VMEM((D, TRI), F32),
    ]
    operands = [
        rel_part.reshape(2, 4, 4, BLK, D),
        neg_part.reshape(2, 2, 8, NEG, D),
        tail_grad, head_grad, ent, ent_state, rel, rel_state, head_ids, asked_tail, asked_neg,
    ]
    number = 1 + 1 + 1 + 1 + 3 + 7 + 3 + 7 + 1 + 3 + 3 + 1
    if more:
        number += 2 + 7 + 1 + 1
        out_shape += [
            jax.ShapeDtypeStruct((TRI, D), BF16),
            jax.ShapeDtypeStruct((2, 2, 8, NEG, D), BF16),
        ]
        scratch += [
            pltpu.VMEM((TRI, D), BF16),
            pltpu.VMEM((NEG, D), BF16),
            pltpu.VMEM((TRI, D), BF16),
            pltpu.VMEM((2, 2, 8, NEG, D), BF16),
        ]
    scratch += [pltpu.SemaphoreType.DMA((number,)), pltpu.SemaphoreType.DMA((number,))]
    return pl.pallas_call(
        functools.partial(update_kernel, bit, more),
        out_shape=tuple(out_shape),
        in_specs=[VMEM_SPEC] * len(operands),
        out_specs=tuple([VMEM_SPEC] * len(out_shape)),
        scratch_shapes=scratch,
        compiler_params=pltpu.CompilerParams(
            collective_id=1 + bit, has_side_effects=True, vmem_limit_bytes=40 << 20
        ),
        name="update",
    )(*operands)


def shards(
    entity_rows, entity_state, relation_rows, relation_state,
    conv_weight, conv_bias, fc_weight, fc_bias,
    head_ids, rel_ids, tail_ids, neg_ids,
):
    ent, ent_state = entity_rows.T, entity_state.reshape(1, ENT)
    rel, rel_state = relation_rows.T, relation_state.reshape(1, REL)
    w_mat = fc_weight.T
    tails, negset, t_mat, bias, asked_tail, asked_neg = fetch_rows(tail_ids, neg_ids, ent, conv_weight, conv_bias)
    for r in range(2):
        head_grad, rel_part, neg_part, tail_grad = block_pass(
            r, head_ids, rel_ids, ent, rel, t_mat, w_mat, bias, fc_bias.reshape(1, D),
            tails, negset.reshape(1024, D),
        )
        out = update(
            r, r == 0, rel_part, neg_part, tail_grad, head_grad,
            ent, ent_state, rel, rel_state, head_ids, asked_tail, asked_neg,
        )
        ent, ent_state, rel, rel_state = out[:4]
        if r == 0:
            tails, negset = out[4:]
    return ent.T, ent_state.reshape(ENT), rel.T, rel_state.reshape(REL)


def solution(mesh):
    both = ("group", "shard")
    in_specs = (
        P(both, None), P(both), P(), P(), P(), P(), P(), P(),
        P(None, both), P(None, both), P(None, both), P(None, both),
    )
    out_specs = (P(both, None), P(both), P(), P())
    return jax.shard_map(shards, mesh=mesh, in_specs=in_specs, out_specs=out_specs, check_vma=False)
```

time: 210 us -> 170 us (0.81)
  Pallas kernels: 178 us -> 143 us
  starting transfers between devices: 4.48 us -> 0 us
  other arithmetic: 3.51 us -> 1.35 us
    pallas_call x4 -> x3, Pallas kernels: 90.2 us -> 66 us  [the longest x2 39 us: block_pass(): pl.pallas_call(functools.partial(pass_kernel, round_index), grid=(2, STEP...]
    pallas_call x2, Pallas kernels: 87.6 us -> 77.1 us  [update(): pl.pallas_call(functools.partial(update_kernel, bit, more), out_shape=tup...]
    unnamed x26 -> x57, local copies, waits for them, and re-layouts: 16.1 us -> 23 us
    ppermute x2 -> x0, starting transfers between devices: 4.48 us -> none  [partner_ids(): return lax.ppermute(ids, 'group', route)]
    reshape x4 -> x1, local copies, waits for them, and re-layouts: 3.67 us -> 0.7 us  [shards(): rel, rel_state = (relation_rows.T, relation_state.reshape(1, REL))]
  transfers between devices with their start and end apart: 2 -> 0, of which waited for: 0 -> 0; matrix products, arithmetic and copies ran while one was open for 9% -> 0% of each run, Pallas kernels for 9% -> 0%
where the time goes in v2:
time: 170 us
  Pallas kernels  143 us (84%)
  local copies, waits for them, and re-layouts  24.5 us (14%)
    pallas_call x2, Pallas kernels, update(): pl.pallas_call(functools.partial(update_kernel, bit, more), out_shape=tup...  77.1 us
    pallas_call x2, Pallas kernels, block_pass(): pl.pallas_call(functools.partial(pass_kernel, round_index), grid=(2, STEP...  39 us
    pallas_call x1, Pallas kernels, fetch_rows(): pl.pallas_call(rows_kernel, out_shape=(jax.ShapeDtypeStruct((TRI, D), BF1...  26.9 us
    unnamed x57, local copies, waits for them, and re-layouts  23 us

profile of v2, /device:TPU:1, one launch (start us, length us, event | category | flops | bytes accessed | tf_op | source)
XLA Modules:
  0.0 169.7 jit_solution(11336099478398041996)
XLA Ops:
  0.6 0.1 pad.2.clone
  0.7 0.7 reshape.50.rel_state
  1.4 0.7 reshape.56
  2.1 0.7 maximum_bitcast_fusion.wb_ref
  2.8 0.0 copy-start.1
  2.8 1.1 copy-done.1
  4.0 0.0 copy-start.14
  4.0 1.0 copy-done.14
  5.0 0.0 copy-start.25
  5.0 0.7 copy-done.25
  5.6 0.0 copy-start.26
  5.6 0.7 copy-done.26
  6.3 26.9 %fetch_rows.1 = (bf16[128,200]{1,0:T(8,128)(2,1)S(1)}, bf16[2,2,8,32,200]{4,3,2,1,0:T(8,128)(2,1)S(1)}, bf16[9,2,240,1152]{3,2,1,0:T(8,128)(2,1)S(1)}, f32[9,1,1...) custom-call(s32[2,128]{1,0:T(2,128)S(1)} %copy-done.25, s32[2,32]{1,0:T(2,128)S(1)} %copy-done.26, ...), custom_call_target="tpu_custom_call" | custom-call | tf_op jit(solution)/shard_map/fetch_rows/pallas_call | solution.py:347
  33.2 0.0 copy-start
  33.2 3.8 %copy-done = bf16[9,2,240,1152]{3,2,1,0:T(8,128)(2,1)} copy-done((bf16[9,2,240,1152]{3,2,1,0:T(8,128)(2,1)}, bf16[9,2,240,1152]{3,2,1,0:T(8,128)(2,1)S(1)}, u32[]{:S(2)}) %copy-start) | copy-done | bytes 9953304
  37.1 0.0 copy-start.11
  37.1 0.8 copy-done.11
  37.9 0.0 copy-start.15
  37.9 0.6 copy-done.15
  38.5 0.0 copy-start.21
  38.5 0.6 copy-done.21
  39.1 0.0 copy-start.2
  39.1 0.0 copy-start.3
  39.1 0.0 copy-start.22
  39.1 0.0 copy-start.24
  39.1 19.5 %block_pass.2 = (f32[200,128]{1,0:T(8,128)}, bf16[1536,200]{1,0:T(8,128)(2,1)}, bf16[1024,200]{1,0:T(8,128)(2,1)}, f32[200,128]{1,0:T(8,128)}) custom-call(s32[2,128]{1,0:T(2,128)} %head_ids.7, s32[2,128]{1,0:T(2,128)} %rel_ids.3, f32[200,1024]{1,0:T(8,128)} %bitcast.19, f32[200,1387]{1,0:T(8,128)} %bitcast.22, bf16[9,2,240,1152]{3,2,1,0:T(8,128)(2,1)} %copy-done, ...), custom_call_target="tpu_custom_call" | custom-call | tf_op jit(solution)/shard_map/block_pass/pallas_call | solution.py:144
  58.6 0.0 copy-done.2
  58.6 0.0 copy-done.3
  58.6 0.0 copy-done.22
  58.6 0.0 copy-done.24
  58.7 0.0 copy-start.9
  58.7 1.1 copy-done.9
  59.8 1.0 copy-done.13
  60.8 0.0 copy-start.18
  60.8 0.9 copy-done.18
  61.7 0.0 copy-start.19
  61.7 0.9 copy-done.19
  62.6 41.2 %update.2 = (f32[200,1024]{1,0:T(8,128)S(1)}, f32[1,1024]{1,0:T(1,128)S(1)}, f32[200,1387]{1,0:T(8,128)S(1)}, f32[1,1387]{1,0:T(1,128)S(1)}, bf16[128,200]{1,0:T...) custom-call(bf16[2,4,4,48,200]{4,3,2,1,0:T(8,128)(2,1)S(1)} %bitcast.27, bf16[2,2,8,32,200]{4,3,2,1,0:T(8,128)(2,1)S(1)} %bitcast.31, ...), custom_call_target="tpu_custom_call" | custom-call | tf_op jit(solution)/shard_map/update/pallas_call | solution.py:560
  103.9 0.0 copy-start.4
  103.9 1.0 copy-done.4
  104.9 0.0 copy-start.6
  104.9 0.9 copy-done.6
  105.8 0.0 copy-start.10
  105.8 0.8 copy-done.10
  106.5 0.0 copy-start.20
  106.5 0.6 copy-done.20
  107.2 0.0 copy-start.5
  107.2 0.0 copy-start.7
  107.2 0.0 copy-start.23
  107.2 19.5 %block_pass.3 = (f32[200,128]{1,0:T(8,128)}, bf16[1536,200]{1,0:T(8,128)(2,1)}, bf16[1024,200]{1,0:T(8,128)(2,1)}, f32[200,128]{1,0:T(8,128)}) custom-call(s32[2,128]{1,0:T(2,128)} %head_ids.7, s32[2,128]{1,0:T(2,128)} %rel_ids.3, f32[200,1024]{1,0:T(8,128)} %copy-done.6, f32[200,1387]{1,0:T(8,128)} %copy-done.4, bf16[9,2,240,1152]{3,2,1,0:T(8,128)(2,1)} %copy-done, ...), custom_call_target="tpu_custom_call" | custom-call | tf_op jit(solution)/shard_map/block_pass/pallas_call | solution.py:144
  126.7 0.0 copy-done.5
  126.7 0.0 copy-done.7
  126.7 0.0 copy-done.23
  126.7 0.0 copy-start.8
  126.8 1.1 copy-done.8
  127.9 0.0 copy-start.12
  127.9 1.0 copy-done.12
  128.9 0.9 copy-done.16
  129.8 0.9 copy-done.17
  130.7 35.9 %update.3 = (f32[200,1024]{1,0:T(8,128)S(1)}, f32[1,1024]{1,0:T(1,128)S(1)}, f32[200,1387]{1,0:T(8,128)S(1)}, f32[1,1387]{1,0:T(1,128)S(1)}) custom-call(bf16[2,4,4,48,200]{4,3,2,1,0:T(8,128)(2,1)S(1)} %bitcast.26, bf16[2,2,8,32,200]{4,3,2,1,0:T(8,128)(2,1)S(1)} %bitcast.30, f32[200,128]{1,0:T(8,128)S(1)} %copy-done.17, f32[200,128]{1,0:T(8,128)S(1)} %copy-done.16, ...), custom_call_target="tpu_custom_call" | custom-call | tf_op jit(solution)/shard_map/update/pallas_call | solution.py:560
  166.6 0.6 reduce
  167.3 0.9 copy.22
  168.2 0.6 copy.23
  168.7 1.0 copy.24
  (4 shorter events, 0.0 us)
Async XLA Ops:
  2.8 1.1 copy-start.1
  4.0 1.0 copy-start.14
  5.0 0.7 copy-start.25
  5.6 0.7 copy-start.26
  33.2 3.8 %copy-start = (bf16[9,2,240,1152]{3,2,1,0:T(8,128)(2,1)}, bf16[9,2,240,1152]{3,2,1,0:T(8,128)(2,1)S(1)}, u32[]{:S(2)}) copy-start(bf16[9,2,240,1152]{3,2,1,0:T(8,128)(2,1)S(1)} %get-tuple-element.28.t_hbm) | copy-start | bytes 29859844
  37.1 0.8 copy-start.11
  37.9 0.6 copy-start.15
  38.5 0.6 copy-start.21
  39.1 19.5 %copy-start.2 = (f32[1024,200]{0,1:T(8,128)S(1)}, f32[1024,200]{0,1:T(8,128)}, u32[]{:S(2)}) copy-start(f32[1024,200]{0,1:T(8,128)} %param.15) | copy-start | bytes 2457604
  39.1 19.5 %copy-start.3 = (f32[1387,200]{0,1:T(8,128)S(1)}, f32[1387,200]{0,1:T(8,128)}, u32[]{:S(2)}) copy-start(f32[1387,200]{0,1:T(8,128)} %param.17) | copy-start | bytes 3328804
  39.1 19.6 %copy-start.22 = (s32[2,128]{1,0:T(2,128)S(1)}, s32[2,128]{1,0:T(2,128)}, u32[]{:S(2)}) copy-start(s32[2,128]{1,0:T(2,128)} %head_ids.7) | copy-start | bytes 3076
  39.1 19.6 %copy-start.24 = (f32[1024]{0:T(1024)S(1)}, f32[1024]{0:T(1024)}, u32[]{:S(2)}) copy-start(f32[1024]{0:T(1024)} %param.16) | copy-start | bytes 12292
  58.7 1.1 copy-start.9
  59.8 1.0 copy-start.13
  60.8 0.9 copy-start.18
  61.7 0.9 copy-start.19
  103.9 1.0 copy-start.4
  104.9 0.9 copy-start.6
  105.8 0.8 copy-start.10
  106.5 0.6 copy-start.20
  107.2 19.5 %copy-start.5 = (f32[200,1387]{1,0:T(8,128)S(1)}, f32[200,1387]{1,0:T(8,128)}, u32[]{:S(2)}) copy-start(f32[200,1387]{1,0:T(8,128)} %copy-done.4) | copy-start | bytes 3328804
  107.2 19.6 %copy-start.7 = (f32[200,1024]{1,0:T(8,128)S(1)}, f32[200,1024]{1,0:T(8,128)}, u32[]{:S(2)}) copy-start(f32[200,1024]{1,0:T(8,128)} %copy-done.6) | copy-start | bytes 2457604
  107.2 19.6 %copy-start.23 = (s32[2,128]{1,0:T(2,128)S(1)}, s32[2,128]{1,0:T(2,128)}, u32[]{:S(2)}) copy-start(s32[2,128]{1,0:T(2,128)} %head_ids.7) | copy-start | bytes 3076
  126.7 1.1 copy-start.8
  127.9 1.0 copy-start.12
  128.9 0.9 copy-start.16
  129.8 0.9 copy-start.17

commit v3 on v0

v3 whole, which is shorter than its diff:
```python
import jax
import jax.numpy as jnp
import numpy as np
from jax import lax
from jax.experimental import pallas as pl
from jax.experimental.pallas import tpu as pltpu
from jax.sharding import PartitionSpec as P

D = 200
FILTERS = 32
FLAT = 10368
REL = 1387
REL_PAD = 1536
BLK = 48
TRI = 128
NEG = 32
ENT = 1024
CHUNK = 1152
STEPS = FLAT // CHUNK
WIDE = 240
MESH = pl.DeviceIdType.MESH
F32 = jnp.float32
BF16 = jnp.bfloat16

negative_weight = 0.03125
learn_rate = 0.5

NT = (((1,), (1,)), ((), ()))


def nn(a, b):
    return jnp.dot(a, b, preferred_element_type=F32)


def nt(a, b):
    return lax.dot_general(a, b, NT, preferred_element_type=F32)


def spread_dot(one_hot, values):
    high = values.astype(BF16)
    low = (values - high.astype(F32)).astype(BF16)
    return nn(one_hot, high) + nn(one_hot, low)


def hot_rows(ids_row, extent):
    where = lax.broadcasted_iota(jnp.int32, (extent, ids_row.shape[1]), 0)
    return jnp.where(where == ids_row, 1.0, 0.0).astype(BF16)


class Place:
    def __init__(self):
        group = lax.axis_index("group")
        shard = lax.axis_index("shard")
        self.x = group % 4
        self.y_hi = group // 4
        self.y_lo = shard // 16
        self.z = (shard // 2) % 8
        self.core = shard % 2
        self.y = self.y_hi * 2 + self.y_lo

    def at(self, x=None, y=None, z=None, core=None):
        x = self.x if x is None else x
        y = self.y if y is None else y
        z = self.z if z is None else z
        core = self.core if core is None else core
        return ((y // 2) * 4 + x, (y % 2) * 16 + z * 2 + core)

    def mate(self):
        return self.at(core=1 - self.core)

    def beside(self):
        return self.at(y=self.y_hi * 2 + 1 - self.y_lo)

    def partner(self, bit):
        if bit == 0:
            return self.at(x=self.x + 1 - 2 * (self.x % 2))
        return self.at(x=(self.x + 2) % 4)


class Copies:
    def __init__(self, send, recv):
        self.send, self.recv, self.used = send, recv, 0

    def start(self, src, dst, device):
        copy = pltpu.make_async_remote_copy(
            src_ref=src,
            dst_ref=dst,
            send_sem=self.send.at[self.used],
            recv_sem=self.recv.at[self.used],
            device_id=device,
            device_id_type=MESH,
        )
        self.used += 1
        copy.start()
        return copy


def greet(peers):
    barrier = pltpu.get_barrier_semaphore()
    for peer in peers:
        pl.semaphore_signal(barrier, inc=1, device_id=peer, device_id_type=MESH)
    pl.semaphore_wait(barrier, len(peers))


def wait_all(copies):
    for copy in copies:
        copy.wait()


def spacing():
    d = np.arange(D)
    out = np.zeros((D, WIDE), np.float32)
    out[d, d // 20 * 24 + d % 20] = 1.0
    return jnp.asarray(out, BF16)


def features():
    q = np.arange(FLAT).reshape(STEPS, 1, CHUNK)
    return jnp.asarray(np.concatenate([q % 324 // 18, q % 18, q // 324], axis=1).astype(np.int32))


def spread_nt(one_hot, values):
    high = values.astype(BF16)
    low = (values - high.astype(F32)).astype(BF16)
    return nt(one_hot, high) + nt(one_hot, low)


def spread_nt_right(values, one_hot):
    high = values.astype(BF16)
    low = (values - high.astype(F32)).astype(BF16)
    return nt(high, one_hot) + nt(low, one_hot)


def step_of(rows, state, gradient):
    state = state + jnp.sum(gradient * gradient, axis=0, keepdims=True) * (1.0 / D)
    return rows - learn_rate * gradient * lax.rsqrt(state), state


def loop(first, last, body):
    def one(j, carry):
        body(j)
        return carry

    lax.fori_loop(first, last, one, 0)


ROUND_SCRATCH = dict(
    tails=pltpu.VMEM((TRI, D), BF16),
    negs=pltpu.VMEM((2, 2, 8, NEG, D), BF16),
    pick_tail=pltpu.VMEM((TRI, D), BF16),
    pick_neg=pltpu.VMEM((NEG, D), BF16),
    neg_part=pltpu.VMEM((2, 2, 8, NEG, D), BF16),
    tail_grad=pltpu.VMEM((D, TRI), F32),
    tail_in=pltpu.VMEM((D, TRI), F32),
    b1=pltpu.VMEM((2, 8, NEG, D), BF16),
    b2_send=pltpu.VMEM((8, NEG, D), BF16),
    b2_recv=pltpu.VMEM((8, NEG, D), BF16),
    b3_send=pltpu.VMEM((8, NEG, D), BF16),
    b3_recv=pltpu.VMEM((7, NEG, D), BF16),
    b4_send=pltpu.VMEM((NEG, D), F32),
    b4_recv=pltpu.VMEM((NEG, D), F32),
    s0_send=pltpu.VMEM((4, 4, BLK, D), BF16),
    s0_recv=pltpu.VMEM((4, 4, BLK, D), BF16),
    s1_send=pltpu.VMEM((4, 4, BLK, D), BF16),
    s1_recv=pltpu.VMEM((3, 4, BLK, D), BF16),
    acc1=pltpu.VMEM((4, BLK, D), F32),
    s2_recv=pltpu.VMEM((3, BLK, D), F32),
    z_buf=pltpu.VMEM((8, BLK, D), BF16),
    g_buf=pltpu.VMEM((2, 4, 4, BLK, D), BF16),
)
SHARED_SCRATCH = dict(
    tails_in=pltpu.VMEM((2, 2, TRI), jnp.int32),
    negs_in=pltpu.VMEM((2, 2, NEG), jnp.int32),
    columns=pltpu.VMEM((3, 24, CHUNK), F32),
    t_all=pltpu.VMEM((STEPS, 2, WIDE, CHUNK), BF16),
    w_all=pltpu.VMEM((STEPS, D, CHUNK), BF16),
    bias=pltpu.VMEM((STEPS, 1, CHUNK), F32),
    slope=pltpu.VMEM((STEPS, TRI, CHUNK), F32),
    pic_h=pltpu.VMEM((TRI, WIDE), BF16),
    pic_r=pltpu.VMEM((TRI, WIDE), BF16),
    acc=pltpu.VMEM((TRI, D), F32),
    grad_h=pltpu.VMEM((TRI, WIDE), F32),
    grad_r=pltpu.VMEM((TRI, WIDE), F32),
    pre2_grad=pltpu.VMEM((TRI, D), BF16),
    own_part=pltpu.VMEM((4, 4, BLK, D), F32),
)
COPIES = 4 + 2 * (2 + 7 + 1 + 1) + 2 * (1 + 1 + 1 + 7 + 1 + 1 + 3 + 3 + 7 + 3 + 3 + 1)


class Bag:
    def __init__(self, names, refs):
        self.__dict__.update(zip(names, refs))


def window_kernel(
    head_ids, rel_ids, tail_ids, neg_ids, ent_in, ent_state_in, rel_in, rel_state_in,
    conv_w, conv_b, w_hbm, fc_bias, place_ref, space_ref,
    ent, ent_state, rel, rel_state, *rest,
):
    own = Bag(SHARED_SCRATCH, rest)
    rest = rest[len(SHARED_SCRATCH):]
    rounds = []
    for r in range(2):
        rounds.append(Bag(ROUND_SCRATCH, rest))
        rest = rest[len(ROUND_SCRATCH):]
    w_sem, send, recv = rest
    me = Place()
    copies = Copies(send, recv)
    c, z, y_lo = me.core, me.z, me.y_lo
    first = me.x * (1 - c) + me.y * c
    second = me.y * (1 - c) + me.x * c

    def along_first(i):
        return me.at(x=i * (1 - c) + me.x * c, y=i * c + me.y * (1 - c))

    def along_second(i):
        return me.at(x=me.x * (1 - c) + i * c, y=i * (1 - c) + me.y * c)

    firsts = [(first + d) % 4 for d in range(1, 4)]
    seconds = [(second + d) % 4 for d in range(1, 4)]
    zs = [(z + d) % 8 for d in range(1, 8)]
    mate, beside = me.mate(), me.beside()
    partners = [me.partner(0), me.partner(1)]

    w_copies = []
    for j in range(STEPS):
        copy = pltpu.make_async_copy(
            w_hbm.at[:, pl.ds(j * CHUNK, CHUNK)], own.w_all.at[j], w_sem.at[j]
        )
        copy.start()
        w_copies.append(copy)
    greet(
        [mate]
        + [along_first(i) for i in firsts]
        + [along_second(i) for i in seconds]
        + [me.at(z=i) for i in zs]
    )
    asked = [
        (
            copies.start(tail_ids, own.tails_in.at[r], partners[r]),
            copies.start(neg_ids, own.negs_in.at[r], partners[r]),
        )
        for r in range(2)
    ]

    def build(j):
        down, across, filt = (place_ref[j, k : k + 1, :] for k in range(3))
        hot = lax.broadcasted_iota(jnp.int32, (FILTERS, CHUNK), 0) == filt
        own.bias[j] = jnp.dot(
            conv_b[...], jnp.where(hot, 1.0, 0.0).astype(F32),
            precision=lax.Precision.HIGHEST, preferred_element_type=F32,
        )
        hot = jnp.where(hot, 1.0, 0.0).astype(BF16)
        apart = lax.broadcasted_iota(jnp.int32, (24, CHUNK), 0) - across
        for a in range(3):
            wide = nn(conv_w[a], hot)
            out = jnp.zeros((24, CHUNK), F32)
            for k in range(3):
                out = jnp.where(apart == k, wide[k : k + 1, :], out)
            own.columns[a] = out
        for half in range(2):

            def pair(p):
                rows = []
                for one in range(2):
                    away = (10 * half + 2 * p + one) - down
                    out = jnp.where(away == 2, own.columns[2], 0.0)
                    out = jnp.where(away == 1, own.columns[1], out)
                    rows.append(jnp.where(away == 0, own.columns[0], out))
                low = pl.multiple_of(p * 48, 48)
                own.t_all[j, half, pl.ds(low, 48), :] = jnp.concatenate(rows, axis=0).astype(BF16)

            loop(0, 5, pair)

    def forward(j):
        pre1 = nn(own.pic_h[...], own.t_all[j, 0]) + nn(own.pic_r[...], own.t_all[j, 1]) + own.bias[j]
        sigma = 0.5 * jnp.tanh(0.5 * pre1) + 0.5
        act = pre1 * sigma
        own.slope[j] = sigma + act * (1.0 - sigma)
        own.acc[...] += nt(act.astype(BF16), own.w_all[j])

    def backward(j):
        act_grad = nn(own.pre2_grad[...], own.w_all[j])
        pre1_grad = (act_grad * own.slope[j]).astype(BF16)
        own.grad_h[...] += nt(pre1_grad, own.t_all[j, 0])
        own.grad_r[...] += nt(pre1_grad, own.t_all[j, 1])

    def pick_heads(r, table):
        heads = nn(table, hot_rows(head_ids[r : r + 1, :], ENT))
        own.pic_h[...] = nn(heads.T.astype(BF16), space_ref[...]).astype(BF16)

    def pick_relations(r, table):
        relations = nn(table, hot_rows(rel_ids[r : r + 1, :], REL))
        own.pic_r[...] = nn(relations.T.astype(BF16), space_ref[...]).astype(BF16)

    def rows_go(r, table):
        b = rounds[r]
        b.pick_neg[...] = nn(table, hot_rows(own.negs_in[r, r : r + 1, :], ENT)).T.astype(BF16)
        b.pick_tail[...] = nn(table, hot_rows(own.tails_in[r, r : r + 1, :], ENT)).T.astype(BF16)
        slot = b.negs.at[c, y_lo, z]
        return (
            copies.start(b.pick_neg, slot, partners[r]),
            copies.start(b.pick_tail, b.tails, partners[r]),
        )

    def negs_along_z(r):
        slot = rounds[r].negs.at[c, y_lo, z]
        return [copies.start(slot, slot, me.at(z=i)) for i in zs]

    def negs_beside(r):
        half = rounds[r].negs.at[c, y_lo]
        return copies.start(half, half, beside)

    def negs_to_mate(r):
        half = rounds[r].negs.at[c]
        return copies.start(half, half, mate)

    loop(0, 2, build)
    for pair in asked:
        wait_all(pair)
    table = ent_in[...].astype(BF16)
    neg_go, tail_go = rows_go(0, table)
    pick_heads(0, table)
    pick_relations(0, rel_in[...].astype(BF16))
    loop(2, 4, build)
    neg_go.wait()
    along = negs_along_z(0)
    loop(4, STEPS, build)
    wait_all(along)
    near = negs_beside(0)
    wait_all(w_copies)
    own.acc[...] = jnp.zeros_like(own.acc)
    loop(0, 5, forward)
    near.wait()
    near = negs_to_mate(0)
    loop(5, STEPS, forward)
    near.wait()
    tail_go.wait()

    for r in range(2):
        b = rounds[r]
        more = r == 0
        if r == 1:
            own.acc[...] = jnp.zeros_like(own.acc)
            loop(0, STEPS, forward)
        pre2 = own.acc[...] + fc_bias[...]
        sigma = jax.nn.sigmoid(pre2)
        query = (pre2 * sigma).astype(BF16)
        tails = b.tails[...].astype(F32)
        wide = query.astype(F32)
        pos_grad = -jax.nn.sigmoid(-jnp.sum(wide * tails, axis=1, keepdims=True))
        negset = b.negs[...].reshape(1024, D)
        by_neg = (negative_weight * jax.nn.sigmoid(nt(negset, query))).astype(BF16)
        b.neg_part[...] = nn(by_neg, query).astype(BF16).reshape(2, 2, 8, NEG, D)
        b1_copy = copies.start(b.neg_part.at[1 - c], b.b1, mate)
        b.tail_grad[...] = (pos_grad * wide).T
        tail_copy = copies.start(b.tail_grad, b.tail_in, partners[r])
        by_row = (negative_weight * jax.nn.sigmoid(nt(query, negset))).astype(BF16)
        query_grad = pos_grad * tails + nn(by_row, negset)
        own.pre2_grad[...] = (query_grad * (sigma * (1.0 + pre2 * (1.0 - sigma)))).astype(BF16)
        own.grad_h[...] = jnp.zeros_like(own.grad_h)
        own.grad_r[...] = jnp.zeros_like(own.grad_r)
        loop(0, 3, backward)
        b1_copy.wait()
        b.b2_send[...] = (b.neg_part[c, 1 - y_lo].astype(F32) + b.b1[1 - y_lo].astype(F32)).astype(BF16)
        b2_copy = copies.start(b.b2_send, b.b2_recv, beside)
        loop(3, 6, backward)
        b2_copy.wait()
        b.b3_send[...] = (
            b.neg_part[c, y_lo].astype(F32) + b.b1[y_lo].astype(F32) + b.b2_recv[...].astype(F32)
        ).astype(BF16)
        b3_copies = [
            copies.start(b.b3_send.at[i], b.b3_recv.at[d], me.at(z=i)) for d, i in enumerate(zs)
        ]
        loop(6, STEPS, backward)
        relation_grad = spread_nt_right(own.grad_r[...], space_ref[...])
        rel_row = rel_ids[r : r + 1, :]
        half = REL_PAD // 2

        def part_of(core):
            where = lax.broadcasted_iota(jnp.int32, (half, TRI), 0) + core * half
            hot = jnp.where(where == rel_row, 1.0, 0.0).astype(BF16)
            return spread_dot(hot, relation_grad).reshape(4, 4, BLK, D)

        b.s0_send[...] = part_of(1 - c).astype(BF16)
        s0_copy = copies.start(b.s0_send, b.s0_recv, mate)
        own.own_part[...] = part_of(c)
        wait_all(b3_copies)
        share = b.b3_send[z].astype(F32)
        for d in range(7):
            share = share + b.b3_recv[d].astype(F32)
        b.b4_send[...] = share
        b4_copy = copies.start(b.b4_send, b.b4_recv, partners[r])
        s0_copy.wait()
        for i in range(4):
            b.s1_send[i] = (own.own_part[i] + b.s0_recv[i].astype(F32)).astype(BF16)
        s1_copies = [
            copies.start(b.s1_send.at[i], b.s1_recv.at[d], along_first(i)) for d, i in enumerate(firsts)
        ]
        head_grad = spread_nt(space_ref[...], own.grad_h[...])
        gradient = spread_nt_right(head_grad, hot_rows(head_ids[r : r + 1, :], ENT))
        tail_copy.wait()
        b4_copy.wait()
        gradient = (
            gradient
            + spread_nt_right(b.tail_in[...], hot_rows(own.tails_in[r, r : r + 1, :], ENT))
            + spread_nt_right(b.b4_recv[...].T, hot_rows(own.negs_in[r, r : r + 1, :], ENT))
        )
        if more:
            new_rows, new_state = step_of(ent_in[...], ent_state_in[...], gradient)
        else:
            new_rows, new_state = step_of(ent[...], ent_state[...], gradient)
        ent[...] = new_rows
        ent_state[...] = new_state
        wait_all(s1_copies)
        b.acc1[...] = (
            own.own_part[first]
            + b.s0_recv[first].astype(F32)
            + b.s1_recv[0].astype(F32)
            + b.s1_recv[1].astype(F32)
            + b.s1_recv[2].astype(F32)
        )
        s2_copies = [
            copies.start(b.acc1.at[i], b.s2_recv.at[d], along_second(i)) for d, i in enumerate(seconds)
        ]
        if more:
            table = ent[...].astype(BF16)
            neg_go, tail_go = rows_go(1, table)
        wait_all(s2_copies)
        b.z_buf[z] = (b.acc1[second] + b.s2_recv[0] + b.s2_recv[1] + b.s2_recv[2]).astype(BF16)
        z_copies = [copies.start(b.z_buf.at[z], b.z_buf.at[z], me.at(z=i)) for i in zs]
        if more:
            pick_heads(1, table)
            neg_go.wait()
            along = negs_along_z(1)
        wait_all(z_copies)
        total = b.z_buf[0].astype(F32)
        for i in range(1, 8):
            total = total + b.z_buf[i].astype(F32)
        b.g_buf[c, first, second] = total.astype(BF16)
        slot = b.g_buf.at[c, first, second]
        s4_copies = [copies.start(slot, slot, along_second(i)) for i in seconds]
        if more:
            wait_all(along)
            near = negs_beside(1)
        wait_all(s4_copies)
        slot = b.g_buf.at[c, first]
        s5_copies = [copies.start(slot, slot, along_first(i)) for i in firsts]
        if more:
            near.wait()
            near = negs_to_mate(1)
        wait_all(s5_copies)
        slot = b.g_buf.at[c]
        s6_copy = copies.start(slot, slot, mate)
        eye = jnp.where(
            lax.broadcasted_iota(jnp.int32, (D, D), 0) == lax.broadcasted_iota(jnp.int32, (D, D), 1), 1.0, 0.0
        ).astype(BF16)
        s6_copy.wait()
        gradient = nt(eye, b.g_buf[...].reshape(REL_PAD, D))[:, :REL]
        if more:
            new_rows, new_state = step_of(rel_in[...], rel_state_in[...], gradient)
        else:
            new_rows, new_state = step_of(rel[...], rel_state[...], gradient)
        rel[...] = new_rows
        rel_state[...] = new_state
        if more:
            pick_relations(1, new_rows.astype(BF16))
            near.wait()
            tail_go.wait()


def shards(
    entity_rows, entity_state, relation_rows, relation_state,
    conv_weight, conv_bias, fc_weight, fc_bias,
    head_ids, rel_ids, tail_ids, neg_ids,
):
    vmem = pl.BlockSpec(memory_space=pltpu.VMEM)
    operands = [
        head_ids, rel_ids, tail_ids, neg_ids,
        entity_rows.T, entity_state.reshape(1, ENT), relation_rows.T, relation_state.reshape(1, REL),
        jnp.transpose(conv_weight, (1, 2, 0)), conv_bias.reshape(1, FILTERS),
        fc_weight.T, fc_bias.reshape(1, D), features(), spacing(),
    ]
    specs = [vmem] * len(operands)
    specs[10] = pl.BlockSpec(memory_space=pl.ANY)
    ent, ent_state, rel, rel_state = pl.pallas_call(
        window_kernel,
        out_shape=(
            jax.ShapeDtypeStruct((D, ENT), F32),
            jax.ShapeDtypeStruct((1, ENT), F32),
            jax.ShapeDtypeStruct((D, REL), F32),
            jax.ShapeDtypeStruct((1, REL), F32),
        ),
        in_specs=specs,
        out_specs=(vmem,) * 4,
        scratch_shapes=[
            *SHARED_SCRATCH.values(),
            *ROUND_SCRATCH.values(),
            *ROUND_SCRATCH.values(),
            pltpu.SemaphoreType.DMA((STEPS,)),
            pltpu.SemaphoreType.DMA((COPIES,)),
            pltpu.SemaphoreType.DMA((COPIES,)),
        ],
        compiler_params=pltpu.CompilerParams(
            collective_id=0, has_side_effects=True, vmem_limit_bytes=60 << 20
        ),
        name="window",
    )(*operands)
    return ent.T, ent_state.reshape(ENT), rel.T, rel_state.reshape(REL)


def solution(mesh):
    both = ("group", "shard")
    in_specs = (
        P(both, None), P(both), P(), P(), P(), P(), P(), P(),
        P(None, both), P(None, both), P(None, both), P(None, both),
    )
    out_specs = (P(both, None), P(both), P(), P())
    return jax.shard_map(shards, mesh=mesh, in_specs=in_specs, out_specs=out_specs, check_vma=False)
```

time: 834 us -> 130 us (0.16); the launches traced: 819 us -> 130 us
  waiting for transfers between devices: 501 us -> 0 us
  Pallas kernels: 0 us -> 123 us
  local copies, waits for them, and re-layouts: 126 us -> 5.01 us
  blocking collectives: 84.4 us -> 0 us
  matrix products: 48.1 us -> 0 us
  other arithmetic: 34.5 us -> 1.4 us
  between operations: 16.4 us -> 0.66 us
  starting transfers between devices: 8.87 us -> 0 us
    psum x2 -> x0, waiting for transfers between devices: 393 us -> none  [shards(): rel_total = lax.psum(rel_part, ('group', 'shard'))]
    pallas_call x0 -> x1, Pallas kernels: none -> 123 us  [shards(): pl.pallas_call(window_kernel, out_shape=(jax.ShapeDtypeStruct((D, ENT), F...]
    unnamed x6 -> x0, waiting for transfers between devices: 98.6 us -> none
    all_gather x2 -> x0, blocking collectives: 84.4 us -> none  [shards(): negset = lax.all_gather(own_negative, 'shard', axis=0, tiled=True)]
    dot_general x10 -> x0, matrix products: 44.6 us -> none  [the longest x2 11.8 us: local_pass(): jnp.einsum('fk,fijt->kijt', filters, pre1_grad, preferred_element_type=jn...]
    reshape x17 -> x1, local copies, waits for them, and re-layouts: 33.8 us -> 1.29 us  [shards(): relation_state.reshape(1, REL)]
    another operation x26 -> x0, local copies, waits for them, and re-layouts: 31.1 us -> none  [the longest x22 27.5 us: local_pass(): jnp.stack([picture[row_off:row_off + height, col_off:col_off + across] fo...]
    gather x14 -> x0, local copies, waits for them, and re-layouts: 18.8 us -> none  [the longest x4 6.17 us: shards(): ent_bf[heads]]
  transfers between devices with their start and end apart: 8 -> 0, of which waited for: 4 -> 0; matrix products, arithmetic and copies ran while one was open for 13% -> 0% of each run, Pallas kernels for 0% -> 0%
where the time goes in v3:
time: 130 us
  Pallas kernels  123 us (95%)
  local copies, waits for them, and re-layouts  5.01 us (4%)
  other arithmetic  1.4 us (1%)
    pallas_call x1, Pallas kernels, shards(): pl.pallas_call(window_kernel, out_shape=(jax.ShapeDtypeStruct((D, ENT), F...  123 us
    unnamed x7, local copies, waits for them, and re-layouts  3.71 us

profile of v3, /device:TPU:1, one launch (start us, length us, event | category | flops | bytes accessed | tf_op | source)
XLA Modules:
  0.0 129.6 jit_solution(16187340266887185805)
XLA Ops:
  0.6 1.3 reshape.27.rel_state_in
  1.9 122.6 %window.1 = (f32[200,1024]{1,0:T(8,128)}, f32[1,1024]{1,0:T(1,128)}, f32[200,1387]{1,0:T(8,128)}, f32[1,1387]{1,0:T(1,128)}) custom-call(s32[2,128]{1,0:T(2,128)} %head_ids.1, s32[2,128]{1,0:T(2,128)} %rel_ids.1, s32[2,128]{1,0:T(2,128)} %tail_ids.1, s32[2,32]{1,0:T(2,128)} %neg_ids.1, f32[200,1024]{1,0:T(8,128)} %bitcast.13, f32[1,1024]{1,0:T(1,128)} %bitcast.15, ...), custom_call_target="tpu_custom_call" | custom-call | tf_op jit(solution)/shard_map/window/pallas_call | solution.py:486
  124.5 0.0 copy-start.1
  124.5 0.0 copy-start
  124.5 1.4 %reduce = f32[1387]{0:T(1024)} reduce(f32[1,1387]{1,0:T(1,128)} %get-tuple-element.11, f32[]{:T(128)} %constant.10), dimensions={0}, to_apply=%get-tuple-element.11.reduce_sub_computation | reduce | bytes 11100 | tf_op jit(solution)/shard_map/window/pallas_call | solution.py:486
  125.9 2.1 %copy.21 = f32[1024,200]{0,1:T(8,128)} copy(f32[1024,200]{0,1:T(8,128)} %bitcast.14) | data formatting | bytes 1638400
  128.0 0.0 copy-done.1
  128.0 0.6 copy.22
  128.6 0.0 copy-done
  128.6 1.0 copy.23
Async XLA Ops:
  124.5 3.5 %copy-start.1 = (f32[1,1024]{1,0:T(1,128)S(1)}, f32[1,1024]{1,0:T(1,128)}, u32[]{:S(2)}) copy-start(f32[1,1024]{1,0:T(1,128)} %get-tuple-element.9) | copy-start | bytes 12292
  124.5 4.1 %copy-start = (f32[200,1387]{1,0:T(8,128)S(1)}, f32[200,1387]{1,0:T(8,128)}, u32[]{:S(2)}) copy-start(f32[200,1387]{1,0:T(8,128)} %get-tuple-element.10) | copy-start | bytes 3328804

commit v4 on v3

--- a/solution.py
+++ b/solution.py
@@ -18,6 +18,7 @@
 CHUNK = 1152
 STEPS = FLAT // CHUNK
 WIDE = 240
+LANES = 256
 MESH = pl.DeviceIdType.MESH
 F32 = jnp.float32
 BF16 = jnp.bfloat16
@@ -109,7 +110,7 @@
 
 def spacing():
     d = np.arange(D)
-    out = np.zeros((D, WIDE), np.float32)
+    out = np.zeros((LANES, WIDE), np.float32)
     out[d, d // 20 * 24 + d % 20] = 1.0
     return jnp.asarray(out, BF16)
 
@@ -136,6 +137,11 @@
     return rows - learn_rate * gradient * lax.rsqrt(state), state
 
 
+def widen():
+    row = lax.broadcasted_iota(jnp.int32, (D, LANES), 0)
+    return jnp.where(row == lax.broadcasted_iota(jnp.int32, (D, LANES), 1), 1.0, 0.0).astype(BF16)
+
+
 def loop(first, last, body):
     def one(j, carry):
         body(j)
@@ -145,28 +151,26 @@
 
 
 ROUND_SCRATCH = dict(
-    tails=pltpu.VMEM((TRI, D), BF16),
-    negs=pltpu.VMEM((2, 2, 8, NEG, D), BF16),
-    pick_tail=pltpu.VMEM((TRI, D), BF16),
-    pick_neg=pltpu.VMEM((NEG, D), BF16),
-    neg_part=pltpu.VMEM((2, 2, 8, NEG, D), BF16),
+    tails=pltpu.VMEM((TRI, LANES), BF16),
+    negs=pltpu.VMEM((2, 2, 8, NEG, LANES), BF16),
+    pick_tail=pltpu.VMEM((TRI, LANES), BF16),
+    pick_neg=pltpu.VMEM((NEG, LANES), BF16),
+    neg_part=pltpu.VMEM((2, 2, 8, NEG, LANES), BF16),
     tail_grad=pltpu.VMEM((D, TRI), F32),
     tail_in=pltpu.VMEM((D, TRI), F32),
-    b1=pltpu.VMEM((2, 8, NEG, D), BF16),
-    b2_send=pltpu.VMEM((8, NEG, D), BF16),
-    b2_recv=pltpu.VMEM((8, NEG, D), BF16),
-    b3_send=pltpu.VMEM((8, NEG, D), BF16),
-    b3_recv=pltpu.VMEM((7, NEG, D), BF16),
-    b4_send=pltpu.VMEM((NEG, D), F32),
-    b4_recv=pltpu.VMEM((NEG, D), F32),
-    s0_send=pltpu.VMEM((4, 4, BLK, D), BF16),
-    s0_recv=pltpu.VMEM((4, 4, BLK, D), BF16),
-    s1_send=pltpu.VMEM((4, 4, BLK, D), BF16),
-    s1_recv=pltpu.VMEM((3, 4, BLK, D), BF16),
-    acc1=pltpu.VMEM((4, BLK, D), F32),
-    s2_recv=pltpu.VMEM((3, BLK, D), F32),
-    z_buf=pltpu.VMEM((8, BLK, D), BF16),
-    g_buf=pltpu.VMEM((2, 4, 4, BLK, D), BF16),
+    b1=pltpu.VMEM((2, 8, NEG, LANES), BF16),
+    b2_send=pltpu.VMEM((8, NEG, LANES), BF16),
+    b2_recv=pltpu.VMEM((8, NEG, LANES), BF16),
+    b3_send=pltpu.VMEM((8, NEG, LANES), BF16),
+    b3_recv=pltpu.VMEM((7, NEG, LANES), BF16),
+    b4_send=pltpu.VMEM((NEG, LANES), F32),
+    b4_recv=pltpu.VMEM((NEG, LANES), F32),
+    s0_send=pltpu.VMEM((4, 4, BLK, LANES), BF16),
+    s0_recv=pltpu.VMEM((4, 4, BLK, LANES), BF16),
+    s1_send=pltpu.VMEM((4, 4, BLK, LANES), BF16),
+    s1_recv=pltpu.VMEM((15, BLK, LANES), BF16),
+    z_buf=pltpu.VMEM((8, BLK, LANES), BF16),
+    g_buf=pltpu.VMEM((2, 4, 4, BLK, LANES), BF16),
 )
 SHARED_SCRATCH = dict(
     tails_in=pltpu.VMEM((2, 2, TRI), jnp.int32),
@@ -174,6 +178,7 @@
     columns=pltpu.VMEM((3, 24, CHUNK), F32),
     t_all=pltpu.VMEM((STEPS, 2, WIDE, CHUNK), BF16),
     w_all=pltpu.VMEM((STEPS, D, CHUNK), BF16),
+    p1=pltpu.VMEM((STEPS, TRI, CHUNK), BF16),
     bias=pltpu.VMEM((STEPS, 1, CHUNK), F32),
     slope=pltpu.VMEM((STEPS, TRI, CHUNK), F32),
     pic_h=pltpu.VMEM((TRI, WIDE), BF16),
@@ -182,9 +187,9 @@
     grad_h=pltpu.VMEM((TRI, WIDE), F32),
     grad_r=pltpu.VMEM((TRI, WIDE), F32),
     pre2_grad=pltpu.VMEM((TRI, D), BF16),
-    own_part=pltpu.VMEM((4, 4, BLK, D), F32),
+    own_part=pltpu.VMEM((4, 4, BLK, LANES), F32),
 )
-COPIES = 4 + 2 * (2 + 7 + 1 + 1) + 2 * (1 + 1 + 1 + 7 + 1 + 1 + 3 + 3 + 7 + 3 + 3 + 1)
+COPIES = 4 + 2 * (2 + 7 + 1 + 1) + 2 * (1 + 1 + 1 + 7 + 1 + 1 + 15 + 7 + 15 + 1)
 
 
 class Bag:
@@ -207,17 +212,11 @@
     me = Place()
     copies = Copies(send, recv)
     c, z, y_lo = me.core, me.z, me.y_lo
-    first = me.x * (1 - c) + me.y * c
-    second = me.y * (1 - c) + me.x * c
-
-    def along_first(i):
-        return me.at(x=i * (1 - c) + me.x * c, y=i * c + me.y * (1 - c))
-
-    def along_second(i):
-        return me.at(x=me.x * (1 - c) + i * c, y=i * (1 - c) + me.y * c)
-
-    firsts = [(first + d) % 4 for d in range(1, 4)]
-    seconds = [(second + d) % 4 for d in range(1, 4)]
+    steps = sorted(
+        ((dx, dy) for dx in range(4) for dy in range(4) if dx or dy),
+        key=lambda d: -min(d[0], 4 - d[0]) - min(d[1], 4 - d[1]),
+    )
+    plane = [((me.x + dx) % 4, (me.y + dy) % 4) for dx, dy in steps]
     zs = [(z + d) % 8 for d in range(1, 8)]
     mate, beside = me.mate(), me.beside()
     partners = [me.partner(0), me.partner(1)]
@@ -231,8 +230,7 @@
         w_copies.append(copy)
     greet(
         [mate]
-        + [along_first(i) for i in firsts]
-        + [along_second(i) for i in seconds]
+        + [me.at(x=i, y=k) for i, k in plane]
         + [me.at(z=i) for i in zs]
     )
     asked = [
@@ -272,8 +270,15 @@
 
             loop(0, 5, pair)
 
-    def forward(j):
-        pre1 = nn(own.pic_h[...], own.t_all[j, 0]) + nn(own.pic_r[...], own.t_all[j, 1]) + own.bias[j]
+    def forward_heads(j):
+        own.slope[j] = nn(own.pic_h[...], own.t_all[j, 0]) + own.bias[j]
+
+    def forward(j, heads=None):
+        pre1 = nn(own.pic_r[...], own.t_all[j, 1])
+        if heads is None:
+            pre1 = pre1 + nn(own.pic_h[...], own.t_all[j, 0]) + own.bias[j]
+        else:
+            pre1 = pre1 + heads[j]
         sigma = 0.5 * jnp.tanh(0.5 * pre1) + 0.5
         act = pre1 * sigma
         own.slope[j] = sigma + act * (1.0 - sigma)
@@ -282,21 +287,26 @@
     def backward(j):
         act_grad = nn(own.pre2_grad[...], own.w_all[j])
         pre1_grad = (act_grad * own.slope[j]).astype(BF16)
-        own.grad_h[...] += nt(pre1_grad, own.t_all[j, 0])
+        own.p1[j] = pre1_grad
         own.grad_r[...] += nt(pre1_grad, own.t_all[j, 1])
+
+    def backward_heads(j):
+        own.grad_h[...] += nt(own.p1[j], own.t_all[j, 0])
 
     def pick_heads(r, table):
         heads = nn(table, hot_rows(head_ids[r : r + 1, :], ENT))
-        own.pic_h[...] = nn(heads.T.astype(BF16), space_ref[...]).astype(BF16)
+        own.pic_h[...] = nn(heads.T.astype(BF16), space_ref[:D, :]).astype(BF16)
 
     def pick_relations(r, table):
         relations = nn(table, hot_rows(rel_ids[r : r + 1, :], REL))
-        own.pic_r[...] = nn(relations.T.astype(BF16), space_ref[...]).astype(BF16)
+        own.pic_r[...] = nn(relations.T.astype(BF16), space_ref[:D, :]).astype(BF16)
 
     def rows_go(r, table):
         b = rounds[r]
-        b.pick_neg[...] = nn(table, hot_rows(own.negs_in[r, r : r + 1, :], ENT)).T.astype(BF16)
-        b.pick_tail[...] = nn(table, hot_rows(own.tails_in[r, r : r + 1, :], ENT)).T.astype(BF16)
+        rows = nn(table, hot_rows(own.negs_in[r, r : r + 1, :], ENT)).T.astype(BF16)
+        b.pick_neg[...] = nn(rows, widen()).astype(BF16)
+        rows = nn(table, hot_rows(own.tails_in[r, r : r + 1, :], ENT)).T.astype(BF16)
+        b.pick_tail[...] = nn(rows, widen()).astype(BF16)
         slot = b.negs.at[c, y_lo, z]
         return (
             copies.start(b.pick_neg, slot, partners[r]),
@@ -342,21 +352,26 @@
         more = r == 0
         if r == 1:
             own.acc[...] = jnp.zeros_like(own.acc)
-            loop(0, STEPS, forward)
+            loop(0, 3, lambda j: forward(j, own.slope))
+            near.wait()
+            near = negs_to_mate(1)
+            loop(3, STEPS, lambda j: forward(j, own.slope))
+            near.wait()
+            tail_go.wait()
         pre2 = own.acc[...] + fc_bias[...]
         sigma = jax.nn.sigmoid(pre2)
-        query = (pre2 * sigma).astype(BF16)
+        query = nn((pre2 * sigma).astype(BF16), widen()).astype(BF16)
         tails = b.tails[...].astype(F32)
         wide = query.astype(F32)
         pos_grad = -jax.nn.sigmoid(-jnp.sum(wide * tails, axis=1, keepdims=True))
-        negset = b.negs[...].reshape(1024, D)
+        negset = b.negs[...].reshape(1024, LANES)
         by_neg = (negative_weight * jax.nn.sigmoid(nt(negset, query))).astype(BF16)
-        b.neg_part[...] = nn(by_neg, query).astype(BF16).reshape(2, 2, 8, NEG, D)
+        b.neg_part[...] = nn(by_neg, query).astype(BF16).reshape(2, 2, 8, NEG, LANES)
         b1_copy = copies.start(b.neg_part.at[1 - c], b.b1, mate)
-        b.tail_grad[...] = (pos_grad * wide).T
+        b.tail_grad[...] = (pos_grad * wide).T[:D]
         tail_copy = copies.start(b.tail_grad, b.tail_in, partners[r])
         by_row = (negative_weight * jax.nn.sigmoid(nt(query, negset))).astype(BF16)
-        query_grad = pos_grad * tails + nn(by_row, negset)
+        query_grad = (pos_grad * tails + nn(by_row, negset))[:, :D]
         own.pre2_grad[...] = (query_grad * (sigma * (1.0 + pre2 * (1.0 - sigma)))).astype(BF16)
         own.grad_h[...] = jnp.zeros_like(own.grad_h)
         own.grad_r[...] = jnp.zeros_like(own.grad_r)
@@ -380,7 +395,7 @@
         def part_of(core):
             where = lax.broadcasted_iota(jnp.int32, (half, TRI), 0) + core * half
             hot = jnp.where(where == rel_row, 1.0, 0.0).astype(BF16)
-            return spread_dot(hot, relation_grad).reshape(4, 4, BLK, D)
+            return spread_dot(hot, relation_grad).reshape(4, 4, BLK, LANES)
 
         b.s0_send[...] = part_of(1 - c).astype(BF16)
         s0_copy = copies.start(b.s0_send, b.s0_recv, mate)
@@ -392,19 +407,20 @@
         b.b4_send[...] = share
         b4_copy = copies.start(b.b4_send, b.b4_recv, partners[r])
         s0_copy.wait()
-        for i in range(4):
-            b.s1_send[i] = (own.own_part[i] + b.s0_recv[i].astype(F32)).astype(BF16)
+        b.s1_send[...] = (own.own_part[...] + b.s0_recv[...].astype(F32)).astype(BF16)
         s1_copies = [
-            copies.start(b.s1_send.at[i], b.s1_recv.at[d], along_first(i)) for d, i in enumerate(firsts)
+            copies.start(b.s1_send.at[i, k], b.s1_recv.at[d], me.at(x=i, y=k))
+            for d, (i, k) in enumerate(plane)
         ]
-        head_grad = spread_nt(space_ref[...], own.grad_h[...])
+        loop(0, STEPS, backward_heads)
+        head_grad = spread_nt(space_ref[:D, :], own.grad_h[...])
         gradient = spread_nt_right(head_grad, hot_rows(head_ids[r : r + 1, :], ENT))
         tail_copy.wait()
         b4_copy.wait()
         gradient = (
             gradient
             + spread_nt_right(b.tail_in[...], hot_rows(own.tails_in[r, r : r + 1, :], ENT))
-            + spread_nt_right(b.b4_recv[...].T, hot_rows(own.negs_in[r, r : r + 1, :], ENT))
+            + spread_nt_right(b.b4_recv[...].T[:D], hot_rows(own.negs_in[r, r : r + 1, :], ENT))
         )
         if more:
             new_rows, new_state = step_of(ent_in[...], ent_state_in[...], gradient)
@@ -413,50 +429,33 @@
         ent[...] = new_rows
         ent_state[...] = new_state
         wait_all(s1_copies)
-        b.acc1[...] = (
-            own.own_part[first]
-            + b.s0_recv[first].astype(F32)
-            + b.s1_recv[0].astype(F32)
-            + b.s1_recv[1].astype(F32)
-            + b.s1_recv[2].astype(F32)
-        )
-        s2_copies = [
-            copies.start(b.acc1.at[i], b.s2_recv.at[d], along_second(i)) for d, i in enumerate(seconds)
-        ]
+        mine = own.own_part[me.x, me.y] + b.s0_recv[me.x, me.y].astype(F32)
+        for d in range(15):
+            mine = mine + b.s1_recv[d].astype(F32)
+        b.z_buf[z] = mine.astype(BF16)
+        z_copies = [copies.start(b.z_buf.at[z], b.z_buf.at[z], me.at(z=i)) for i in zs]
         if more:
             table = ent[...].astype(BF16)
             neg_go, tail_go = rows_go(1, table)
-        wait_all(s2_copies)
-        b.z_buf[z] = (b.acc1[second] + b.s2_recv[0] + b.s2_recv[1] + b.s2_recv[2]).astype(BF16)
-        z_copies = [copies.start(b.z_buf.at[z], b.z_buf.at[z], me.at(z=i)) for i in zs]
-        if more:
             pick_heads(1, table)
             neg_go.wait()
             along = negs_along_z(1)
+            loop(0, STEPS, forward_heads)
         wait_all(z_copies)
         total = b.z_buf[0].astype(F32)
         for i in range(1, 8):
             total = total + b.z_buf[i].astype(F32)
-        b.g_buf[c, first, second] = total.astype(BF16)
-        slot = b.g_buf.at[c, first, second]
-        s4_copies = [copies.start(slot, slot, along_second(i)) for i in seconds]
+        b.g_buf[c, me.x, me.y] = total.astype(BF16)
+        slot = b.g_buf.at[c, me.x, me.y]
+        s4_copies = [copies.start(slot, slot, me.at(x=i, y=k)) for i, k in plane]
         if more:
             wait_all(along)
             near = negs_beside(1)
         wait_all(s4_copies)
-        slot = b.g_buf.at[c, first]
-        s5_copies = [copies.start(slot, slot, along_first(i)) for i in firsts]
-        if more:
-            near.wait()
-            near = negs_to_mate(1)
-        wait_all(s5_copies)
         slot = b.g_buf.at[c]
         s6_copy = copies.start(slot, slot, mate)
-        eye = jnp.where(
-            lax.broadcasted_iota(jnp.int32, (D, D), 0) == lax.broadcasted_iota(jnp.int32, (D, D), 1), 1.0, 0.0
-        ).astype(BF16)
         s6_copy.wait()
-        gradient = nt(eye, b.g_buf[...].reshape(REL_PAD, D))[:, :REL]
+        gradient = nt(widen(), b.g_buf[...].reshape(REL_PAD, LANES))[:, :REL]
         if more:
             new_rows, new_state = step_of(rel_in[...], rel_state_in[...], gradient)
         else:
@@ -465,8 +464,6 @@
         rel_state[...] = new_state
         if more:
             pick_relations(1, new_rows.astype(BF16))
-            near.wait()
-            tail_go.wait()
 
 
 def shards(

time: 130 us -> 117 us (0.900)
  Pallas kernels: 123 us -> 109 us
    pallas_call x1, Pallas kernels: 123 us -> 109 us  [shards(): pl.pallas_call(window_kernel, out_shape=(jax.ShapeDtypeStruct((D, ENT), F...]
where the time goes in v4:
time: 117 us; the launch traced here: 116 us
  Pallas kernels  109 us (93%)
  local copies, waits for them, and re-layouts  5.01 us (4%)
  other arithmetic  1.4 us (1%)
    pallas_call x1, Pallas kernels, shards(): pl.pallas_call(window_kernel, out_shape=(jax.ShapeDtypeStruct((D, ENT), F...  109 us
    unnamed x7, local copies, waits for them, and re-layouts  3.71 us

profile of v4, /device:TPU:1, one launch (start us, length us, event | category | flops | bytes accessed | tf_op | source)
XLA Modules:
  0.0 116.3 jit_solution(10444554193179243250)
XLA Ops:
  0.6 1.3 %reshape.27.rel_state_in = f32[1,1387]{1,0:T(1,128)} reshape(f32[1387]{0:T(1024)} %param.17) | data formatting | bytes 11096 | tf_op jit(solution)/shard_map/reshape | solution.py:477
  1.9 109.3 %window.1 = (f32[200,1024]{1,0:T(8,128)}, f32[1,1024]{1,0:T(1,128)}, f32[200,1387]{1,0:T(8,128)}, f32[1,1387]{1,0:T(1,128)}) custom-call(s32[2,128]{1,0:T(2,128)} %head_ids.1, s32[2,128]{1,0:T(2,128)} %rel_ids.1, s32[2,128]{1,0:T(2,128)} %tail_ids.1, s32[2,32]{1,0:T(2,128)} %neg_ids.1, f32[200,1024]{1,0:T(8,128)} %bitcast.14, f32[1,1024]{1,0:T(1,128)} %bitcast.16, ...), custom_call_target="tpu_custom_call" | custom-call | tf_op jit(solution)/shard_map/window/pallas_call | solution.py:483
  111.2 0.0 copy-start.1
  111.2 0.0 copy-start
  111.2 1.4 %reduce = f32[1387]{0:T(1024)} reduce(f32[1,1387]{1,0:T(1,128)} %get-tuple-element.11, f32[]{:T(128)} %constant.10), dimensions={0}, to_apply=%get-tuple-element.11.reduce_sub_computation | reduce | bytes 11100 | tf_op jit(solution)/shard_map/window/pallas_call | solution.py:483
  112.6 2.1 %copy.21 = f32[1024,200]{0,1:T(8,128)} copy(f32[1024,200]{0,1:T(8,128)} %bitcast.13) | data formatting | bytes 1638400
  114.7 0.0 copy-done.1
  114.7 0.6 copy.22
  115.3 0.0 copy-done
  115.3 1.0 copy.23
Async XLA Ops:
  111.2 3.5 %copy-start.1 = (f32[1,1024]{1,0:T(1,128)S(1)}, f32[1,1024]{1,0:T(1,128)}, u32[]{:S(2)}) copy-start(f32[1,1024]{1,0:T(1,128)} %get-tuple-element.9) | copy-start | bytes 12292
  111.2 4.1 %copy-start = (f32[200,1387]{1,0:T(8,128)S(1)}, f32[200,1387]{1,0:T(8,128)}, u32[]{:S(2)}) copy-start(f32[200,1387]{1,0:T(8,128)} %get-tuple-element.10) | copy-start | bytes 3328804

commit v5 on v4

--- a/solution.py
+++ b/solution.py
@@ -167,10 +167,10 @@
     b4_recv=pltpu.VMEM((NEG, LANES), F32),
     s0_send=pltpu.VMEM((4, 4, BLK, LANES), BF16),
     s0_recv=pltpu.VMEM((4, 4, BLK, LANES), BF16),
-    s1_send=pltpu.VMEM((4, 4, BLK, LANES), BF16),
-    s1_recv=pltpu.VMEM((15, BLK, LANES), BF16),
-    z_buf=pltpu.VMEM((8, BLK, LANES), BF16),
-    g_buf=pltpu.VMEM((2, 4, 4, BLK, LANES), BF16),
+    s1_send=pltpu.VMEM((2, 4, 4, BLK, 128), BF16),
+    s1_recv=pltpu.VMEM((2, 15, BLK, 128), BF16),
+    z_buf=pltpu.VMEM((2, 8, BLK, 128), BF16),
+    g_buf=pltpu.VMEM((2, 2, 4, 4, BLK, 128), BF16),
 )
 SHARED_SCRATCH = dict(
     tails_in=pltpu.VMEM((2, 2, TRI), jnp.int32),
@@ -188,8 +188,9 @@
     grad_r=pltpu.VMEM((TRI, WIDE), F32),
     pre2_grad=pltpu.VMEM((TRI, D), BF16),
     own_part=pltpu.VMEM((4, 4, BLK, LANES), F32),
+    ent_grad=pltpu.VMEM((D, ENT), F32),
 )
-COPIES = 4 + 2 * (2 + 7 + 1 + 1) + 2 * (1 + 1 + 1 + 7 + 1 + 1 + 15 + 7 + 15 + 1)
+COPIES = 4 + 2 * (1 + 8 + 1 + 1) + 2 * (1 + 1 + 1 + 7 + 1 + 1 + 2 * (15 + 7 + 15 + 1))
 
 
 class Bag:
@@ -220,6 +221,10 @@
     zs = [(z + d) % 8 for d in range(1, 8)]
     mate, beside = me.mate(), me.beside()
     partners = [me.partner(0), me.partner(1)]
+    across = [
+        lambda i: me.at(x=me.x + 1 - 2 * (me.x % 2), z=i),
+        lambda i: me.at(x=(me.x + 2) % 4, z=i),
+    ]
 
     w_copies = []
     for j in range(STEPS):
@@ -232,6 +237,7 @@
         [mate]
         + [me.at(x=i, y=k) for i, k in plane]
         + [me.at(z=i) for i in zs]
+        + [at(i) for at in across for i in zs]
     )
     asked = [
         (
@@ -309,13 +315,9 @@
         b.pick_tail[...] = nn(rows, widen()).astype(BF16)
         slot = b.negs.at[c, y_lo, z]
         return (
-            copies.start(b.pick_neg, slot, partners[r]),
+            [copies.start(b.pick_neg, slot, across[r](i)) for i in zs + [z]],
             copies.start(b.pick_tail, b.tails, partners[r]),
         )
-
-    def negs_along_z(r):
-        slot = rounds[r].negs.at[c, y_lo, z]
-        return [copies.start(slot, slot, me.at(z=i)) for i in zs]
 
     def negs_beside(r):
         half = rounds[r].negs.at[c, y_lo]
@@ -329,13 +331,10 @@
     for pair in asked:
         wait_all(pair)
     table = ent_in[...].astype(BF16)
-    neg_go, tail_go = rows_go(0, table)
+    along, tail_go = rows_go(0, table)
     pick_heads(0, table)
     pick_relations(0, rel_in[...].astype(BF16))
-    loop(2, 4, build)
-    neg_go.wait()
-    along = negs_along_z(0)
-    loop(4, STEPS, build)
+    loop(2, STEPS, build)
     wait_all(along)
     near = negs_beside(0)
     wait_all(w_copies)
@@ -352,10 +351,7 @@
         more = r == 0
         if r == 1:
             own.acc[...] = jnp.zeros_like(own.acc)
-            loop(0, 3, lambda j: forward(j, own.slope))
-            near.wait()
-            near = negs_to_mate(1)
-            loop(3, STEPS, lambda j: forward(j, own.slope))
+            loop(0, STEPS, lambda j: forward(j, own.slope))
             near.wait()
             tail_go.wait()
         pre2 = own.acc[...] + fc_bias[...]
@@ -379,7 +375,31 @@
         b1_copy.wait()
         b.b2_send[...] = (b.neg_part[c, 1 - y_lo].astype(F32) + b.b1[1 - y_lo].astype(F32)).astype(BF16)
         b2_copy = copies.start(b.b2_send, b.b2_recv, beside)
-        loop(3, 6, backward)
+        loop(3, STEPS, backward)
+        relation_grad = spread_nt_right(own.grad_r[...], space_ref[...])
+        rel_row = rel_ids[r : r + 1, :]
+        half = REL_PAD // 2
+
+        def part_of(core):
+            where = lax.broadcasted_iota(jnp.int32, (half, TRI), 0) + core * half
+            hot = jnp.where(where == rel_row, 1.0, 0.0).astype(BF16)
+            return spread_dot(hot, relation_grad).reshape(4, 4, BLK, LANES)
+
+        b.s0_send[...] = part_of(1 - c).astype(BF16)
+        s0_copy = copies.start(b.s0_send, b.s0_recv, mate)
+        own.own_part[...] = part_of(c)
+        s0_copy.wait()
+        joined = own.own_part[...] + b.s0_recv[...].astype(F32)
+        own.own_part[...] = joined
+        s1_copies = []
+        for h in range(2):
+            b.s1_send[h] = joined[..., h * 128 : h * 128 + 128].astype(BF16)
+            s1_copies.append(
+                [
+                    copies.start(b.s1_send.at[h, i, k], b.s1_recv.at[h, d], me.at(x=i, y=k))
+                    for d, (i, k) in enumerate(plane)
+                ]
+            )
         b2_copy.wait()
         b.b3_send[...] = (
             b.neg_part[c, y_lo].astype(F32) + b.b1[y_lo].astype(F32) + b.b2_recv[...].astype(F32)
@@ -387,40 +407,29 @@
         b3_copies = [
             copies.start(b.b3_send.at[i], b.b3_recv.at[d], me.at(z=i)) for d, i in enumerate(zs)
         ]
-        loop(6, STEPS, backward)
-        relation_grad = spread_nt_right(own.grad_r[...], space_ref[...])
-        rel_row = rel_ids[r : r + 1, :]
-        half = REL_PAD // 2
-
-        def part_of(core):
-            where = lax.broadcasted_iota(jnp.int32, (half, TRI), 0) + core * half
-            hot = jnp.where(where == rel_row, 1.0, 0.0).astype(BF16)
-            return spread_dot(hot, relation_grad).reshape(4, 4, BLK, LANES)
-
-        b.s0_send[...] = part_of(1 - c).astype(BF16)
-        s0_copy = copies.start(b.s0_send, b.s0_recv, mate)
-        own.own_part[...] = part_of(c)
+        loop(0, STEPS, backward_heads)
+        head_grad = spread_nt(space_ref[:D, :], own.grad_h[...])
+        own.ent_grad[...] = spread_nt_right(head_grad, hot_rows(head_ids[r : r + 1, :], ENT))
         wait_all(b3_copies)
         share = b.b3_send[z].astype(F32)
         for d in range(7):
             share = share + b.b3_recv[d].astype(F32)
         b.b4_send[...] = share
         b4_copy = copies.start(b.b4_send, b.b4_recv, partners[r])
-        s0_copy.wait()
-        b.s1_send[...] = (own.own_part[...] + b.s0_recv[...].astype(F32)).astype(BF16)
-        s1_copies = [
-            copies.start(b.s1_send.at[i, k], b.s1_recv.at[d], me.at(x=i, y=k))
-            for d, (i, k) in enumerate(plane)
-        ]
-        loop(0, STEPS, backward_heads)
-        head_grad = spread_nt(space_ref[:D, :], own.grad_h[...])
-        gradient = spread_nt_right(head_grad, hot_rows(head_ids[r : r + 1, :], ENT))
+        z_copies = []
+        for h in range(2):
+            wait_all(s1_copies[h])
+            mine = own.own_part[me.x, me.y][:, h * 128 : h * 128 + 128]
+            for d in range(15):
+                mine = mine + b.s1_recv[h, d].astype(F32)
+            b.z_buf[h, z] = mine.astype(BF16)
+            slot = b.z_buf.at[h, z]
+            z_copies.append([copies.start(slot, slot, me.at(z=i)) for i in zs])
         tail_copy.wait()
+        own.ent_grad[...] += spread_nt_right(b.tail_in[...], hot_rows(own.tails_in[r, r : r + 1, :], ENT))
         b4_copy.wait()
-        gradient = (
-            gradient
-            + spread_nt_right(b.tail_in[...], hot_rows(own.tails_in[r, r : r + 1, :], ENT))
-            + spread_nt_right(b.b4_recv[...].T[:D], hot_rows(own.negs_in[r, r : r + 1, :], ENT))
+        gradient = own.ent_grad[...] + spread_nt_right(
+            b.b4_recv[...].T[:D], hot_rows(own.negs_in[r, r : r + 1, :], ENT)
         )
         if more:
             new_rows, new_state = step_of(ent_in[...], ent_state_in[...], gradient)
@@ -428,40 +437,42 @@
             new_rows, new_state = step_of(ent[...], ent_state[...], gradient)
         ent[...] = new_rows
         ent_state[...] = new_state
-        wait_all(s1_copies)
-        mine = own.own_part[me.x, me.y] + b.s0_recv[me.x, me.y].astype(F32)
-        for d in range(15):
-            mine = mine + b.s1_recv[d].astype(F32)
-        b.z_buf[z] = mine.astype(BF16)
-        z_copies = [copies.start(b.z_buf.at[z], b.z_buf.at[z], me.at(z=i)) for i in zs]
         if more:
             table = ent[...].astype(BF16)
-            neg_go, tail_go = rows_go(1, table)
+            along, tail_go = rows_go(1, table)
             pick_heads(1, table)
-            neg_go.wait()
-            along = negs_along_z(1)
+        s4_copies = []
+        for h in range(2):
+            wait_all(z_copies[h])
+            total = b.z_buf[h, 0].astype(F32)
+            for i in range(1, 8):
+                total = total + b.z_buf[h, i].astype(F32)
+            b.g_buf[h, c, me.x, me.y] = total.astype(BF16)
+            slot = b.g_buf.at[h, c, me.x, me.y]
+            s4_copies.append([copies.start(slot, slot, me.at(x=i, y=k)) for i, k in plane])
+        if more:
             loop(0, STEPS, forward_heads)
-        wait_all(z_copies)
-        total = b.z_buf[0].astype(F32)
-        for i in range(1, 8):
-            total = total + b.z_buf[i].astype(F32)
-        b.g_buf[c, me.x, me.y] = total.astype(BF16)
-        slot = b.g_buf.at[c, me.x, me.y]
-        s4_copies = [copies.start(slot, slot, me.at(x=i, y=k)) for i, k in plane]
-        if more:
             wait_all(along)
             near = negs_beside(1)
-        wait_all(s4_copies)
-        slot = b.g_buf.at[c]
-        s6_copy = copies.start(slot, slot, mate)
-        s6_copy.wait()
-        gradient = nt(widen(), b.g_buf[...].reshape(REL_PAD, LANES))[:, :REL]
+        s6_copies = []
+        for h in range(2):
+            wait_all(s4_copies[h])
+            slot = b.g_buf.at[h, c]
+            s6_copies.append(copies.start(slot, slot, mate))
         if more:
-            new_rows, new_state = step_of(rel_in[...], rel_state_in[...], gradient)
+            near.wait()
+            near = negs_to_mate(1)
+        wait_all(s6_copies)
+        wide = widen()
+        gradient = (
+            nt(wide[:, :128], b.g_buf[0].reshape(REL_PAD, 128)) + nt(wide[:, 128:], b.g_buf[1].reshape(REL_PAD, 128))
+        )[:, :REL]
+        if more:
+            new_rows, new_state = step_of(rel_in[...], rel_state_in[...].reshape(1, REL), gradient)
         else:
-            new_rows, new_state = step_of(rel[...], rel_state[...], gradient)
+            new_rows, new_state = step_of(rel[...], rel_state[...].reshape(1, REL), gradient)
         rel[...] = new_rows
-        rel_state[...] = new_state
+        rel_state[...] = new_state.reshape(REL)
         if more:
             pick_relations(1, new_rows.astype(BF16))
 
@@ -474,7 +485,7 @@
     vmem = pl.BlockSpec(memory_space=pltpu.VMEM)
     operands = [
         head_ids, rel_ids, tail_ids, neg_ids,
-        entity_rows.T, entity_state.reshape(1, ENT), relation_rows.T, relation_state.reshape(1, REL),
+        entity_rows.T, entity_state.reshape(1, ENT), relation_rows.T, relation_state,
         jnp.transpose(conv_weight, (1, 2, 0)), conv_bias.reshape(1, FILTERS),
         fc_weight.T, fc_bias.reshape(1, D), features(), spacing(),
     ]
@@ -486,7 +497,7 @@
             jax.ShapeDtypeStruct((D, ENT), F32),
             jax.ShapeDtypeStruct((1, ENT), F32),
             jax.ShapeDtypeStruct((D, REL), F32),
-            jax.ShapeDtypeStruct((1, REL), F32),
+            jax.ShapeDtypeStruct((REL,), F32),
         ),
         in_specs=specs,
         out_specs=(vmem,) * 4,
@@ -503,7 +514,7 @@
         ),
         name="window",
     )(*operands)
-    return ent.T, ent_state.reshape(ENT), rel.T, rel_state.reshape(REL)
+    return ent.T, ent_state.reshape(ENT), rel.T, rel_state
 
 
 def solution(mesh):

time: 117 us -> 108 us (0.923)
  Pallas kernels: 109 us -> 102 us
  other arithmetic: 1.4 us -> 0 us
    pallas_call x1, Pallas kernels: 109 us -> 102 us  [shards(): pl.pallas_call(window_kernel, out_shape=(jax.ShapeDtypeStruct((D, ENT), F...]
    pallas_call x1 -> x0, other arithmetic: 1.4 us -> none  [shards(): pl.pallas_call(window_kernel, out_shape=(jax.ShapeDtypeStruct((D, ENT), F...]
    reshape x1 -> x0, local copies, waits for them, and re-layouts: 1.29 us -> none  [shards(): relation_state.reshape(1, REL)]
    unnamed x7 -> x10, local copies, waits for them, and re-layouts: 3.71 us -> 4.41 us
where the time goes in v5:
time: 108 us
  Pallas kernels  102 us (94%)
  local copies, waits for them, and re-layouts  4.41 us (4%)
    pallas_call x1, Pallas kernels, shards(): pl.pallas_call(window_kernel, out_shape=(jax.ShapeDtypeStruct((D, ENT), F...  102 us
    unnamed x10, local copies, waits for them, and re-layouts  4.41 us

profile of v5, /device:TPU:1, one launch (start us, length us, event | category | flops | bytes accessed | tf_op | source)
XLA Modules:
  0.0 107.5 jit_solution(5687870892753092703)
XLA Ops:
  0.6 102.4 %window.1 = (f32[200,1024]{1,0:T(8,128)}, f32[1,1024]{1,0:T(1,128)}, f32[200,1387]{1,0:T(8,128)}, f32[1387]{0:T(1024)}) custom-call(s32[2,128]{1,0:T(2,128)} %head_ids.1, s32[2,128]{1,0:T(2,128)} %rel_ids.1, s32[2,128]{1,0:T(2,128)} %tail_ids.1, s32[2,32]{1,0:T(2,128)} %neg_ids.1, f32[200,1024]{1,0:T(8,128)} %bitcast.14, f32[1,1024]{1,0:T(1,128)} %bitcast.16, ...), custom_call_target="tpu_custom_call" | custom-call | tf_op jit(solution)/shard_map/window/pallas_call | solution.py:494
  103.1 0.0 copy-start.2
  103.1 0.0 copy-start
  103.1 2.2 %copy.22 = f32[1024,200]{0,1:T(8,128)} copy(f32[1024,200]{0,1:T(8,128)} %bitcast.13) | data formatting | bytes 1638400
  105.3 0.0 copy-done.2
  105.3 0.6 copy.23
  105.9 0.0 copy-done
  105.9 0.0 copy-start.1
  105.9 1.0 copy.24
  106.9 0.0 copy-done.1
  106.9 0.6 copy.25
Async XLA Ops:
  103.1 2.2 %copy-start.2 = (f32[1,1024]{1,0:T(1,128)S(1)}, f32[1,1024]{1,0:T(1,128)}, u32[]{:S(2)}) copy-start(f32[1,1024]{1,0:T(1,128)} %get-tuple-element.9) | copy-start | bytes 12292
  103.1 2.8 %copy-start = (f32[200,1387]{1,0:T(8,128)S(1)}, f32[200,1387]{1,0:T(8,128)}, u32[]{:S(2)}) copy-start(f32[200,1387]{1,0:T(8,128)} %get-tuple-element.10) | copy-start | bytes 3328804
  105.9 1.0 copy-start.1

commit v6 on v5

--- a/solution.py
+++ b/solution.py
@@ -100,7 +100,7 @@
     barrier = pltpu.get_barrier_semaphore()
     for peer in peers:
         pl.semaphore_signal(barrier, inc=1, device_id=peer, device_id_type=MESH)
-    pl.semaphore_wait(barrier, len(peers))
+    return lambda: pl.semaphore_wait(barrier, len(peers))
 
 
 def wait_all(copies):
@@ -189,6 +189,8 @@
     pre2_grad=pltpu.VMEM((TRI, D), BF16),
     own_part=pltpu.VMEM((4, 4, BLK, LANES), F32),
     ent_grad=pltpu.VMEM((D, ENT), F32),
+    ent=pltpu.VMEM((D, ENT), F32),
+    rel=pltpu.VMEM((D, REL), F32),
 )
 COPIES = 4 + 2 * (1 + 8 + 1 + 1) + 2 * (1 + 1 + 1 + 7 + 1 + 1 + 2 * (15 + 7 + 15 + 1))
 
@@ -199,9 +201,9 @@
 
 
 def window_kernel(
-    head_ids, rel_ids, tail_ids, neg_ids, ent_in, ent_state_in, rel_in, rel_state_in,
+    head_ids, rel_ids, tail_ids, neg_ids, ent_hbm, ent_state_in, rel_hbm, rel_state_in,
     conv_w, conv_b, w_hbm, fc_bias, place_ref, space_ref,
-    ent, ent_state, rel, rel_state, *rest,
+    ent_out, ent_state, rel, rel_state, *rest,
 ):
     own = Bag(SHARED_SCRATCH, rest)
     rest = rest[len(SHARED_SCRATCH):]
@@ -226,6 +228,17 @@
         lambda i: me.at(x=(me.x + 2) % 4, z=i),
     ]
 
+    peers = (
+        [mate]
+        + [me.at(x=i, y=k) for i, k in plane]
+        + [me.at(z=i) for i in zs]
+        + [at(i) for at in across for i in zs]
+    )
+    all_here = greet(peers)
+    ent_copy = pltpu.make_async_copy(ent_hbm, own.ent, w_sem.at[STEPS])
+    rel_copy = pltpu.make_async_copy(rel_hbm, own.rel, w_sem.at[STEPS + 1])
+    ent_copy.start()
+    rel_copy.start()
     w_copies = []
     for j in range(STEPS):
         copy = pltpu.make_async_copy(
@@ -233,20 +246,6 @@
         )
         copy.start()
         w_copies.append(copy)
-    greet(
-        [mate]
-        + [me.at(x=i, y=k) for i, k in plane]
-        + [me.at(z=i) for i in zs]
-        + [at(i) for at in across for i in zs]
-    )
-    asked = [
-        (
-            copies.start(tail_ids, own.tails_in.at[r], partners[r]),
-            copies.start(neg_ids, own.negs_in.at[r], partners[r]),
-        )
-        for r in range(2)
-    ]
-
     def build(j):
         down, across, filt = (place_ref[j, k : k + 1, :] for k in range(3))
         hot = lax.broadcasted_iota(jnp.int32, (FILTERS, CHUNK), 0) == filt
@@ -327,22 +326,33 @@
         half = rounds[r].negs.at[c]
         return copies.start(half, half, mate)
 
-    loop(0, 2, build)
+    loop(0, 4, build)
+    all_here()
+    asked = [
+        (
+            copies.start(tail_ids, own.tails_in.at[r], partners[r]),
+            copies.start(neg_ids, own.negs_in.at[r], partners[r]),
+        )
+        for r in range(2)
+    ]
+    ent_copy.wait()
+    table = own.ent[...].astype(BF16)
+    pick_heads(0, table)
+    loop(4, 7, build)
     for pair in asked:
         wait_all(pair)
-    table = ent_in[...].astype(BF16)
     along, tail_go = rows_go(0, table)
-    pick_heads(0, table)
-    pick_relations(0, rel_in[...].astype(BF16))
-    loop(2, STEPS, build)
-    wait_all(along)
-    near = negs_beside(0)
+    loop(7, STEPS, build)
+    rel_copy.wait()
+    pick_relations(0, own.rel[...].astype(BF16))
     wait_all(w_copies)
     own.acc[...] = jnp.zeros_like(own.acc)
     loop(0, 5, forward)
+    wait_all(along)
+    near = negs_beside(0)
+    loop(5, STEPS, forward)
     near.wait()
     near = negs_to_mate(0)
-    loop(5, STEPS, forward)
     near.wait()
     tail_go.wait()
 
@@ -431,14 +441,14 @@
         gradient = own.ent_grad[...] + spread_nt_right(
             b.b4_recv[...].T[:D], hot_rows(own.negs_in[r, r : r + 1, :], ENT)
         )
+        new_rows, new_state = step_of(own.ent[...], (ent_state_in if more else ent_state)[...], gradient)
+        own.ent[...] = new_rows
+        ent_state[...] = new_state
+        if not more:
+            ent_copy = pltpu.make_async_copy(own.ent, ent_out, w_sem.at[STEPS])
+            ent_copy.start()
         if more:
-            new_rows, new_state = step_of(ent_in[...], ent_state_in[...], gradient)
-        else:
-            new_rows, new_state = step_of(ent[...], ent_state[...], gradient)
-        ent[...] = new_rows
-        ent_state[...] = new_state
-        if more:
-            table = ent[...].astype(BF16)
+            table = own.ent[...].astype(BF16)
             along, tail_go = rows_go(1, table)
             pick_heads(1, table)
         s4_copies = []
@@ -467,11 +477,13 @@
         gradient = (
             nt(wide[:, :128], b.g_buf[0].reshape(REL_PAD, 128)) + nt(wide[:, 128:], b.g_buf[1].reshape(REL_PAD, 128))
         )[:, :REL]
+        old_state = (rel_state_in if more else rel_state)[...].reshape(1, REL)
+        new_rows, new_state = step_of(own.rel[...], old_state, gradient)
         if more:
-            new_rows, new_state = step_of(rel_in[...], rel_state_in[...].reshape(1, REL), gradient)
+            own.rel[...] = new_rows
         else:
-            new_rows, new_state = step_of(rel[...], rel_state[...].reshape(1, REL), gradient)
-        rel[...] = new_rows
+            rel[...] = new_rows
+            ent_copy.wait()
         rel_state[...] = new_state.reshape(REL)
         if more:
             pick_relations(1, new_rows.astype(BF16))
@@ -490,7 +502,8 @@
         fc_weight.T, fc_bias.reshape(1, D), features(), spacing(),
     ]
     specs = [vmem] * len(operands)
-    specs[10] = pl.BlockSpec(memory_space=pl.ANY)
+    far = pl.BlockSpec(memory_space=pltpu.HBM)
+    specs[4] = specs[6] = specs[10] = far
     ent, ent_state, rel, rel_state = pl.pallas_call(
         window_kernel,
         out_shape=(
@@ -500,12 +513,12 @@
             jax.ShapeDtypeStruct((REL,), F32),
         ),
         in_specs=specs,
-        out_specs=(vmem,) * 4,
+        out_specs=(far, vmem, vmem, vmem),
         scratch_shapes=[
             *SHARED_SCRATCH.values(),
             *ROUND_SCRATCH.values(),
             *ROUND_SCRATCH.values(),
-            pltpu.SemaphoreType.DMA((STEPS,)),
+            pltpu.SemaphoreType.DMA((STEPS + 2,)),
             pltpu.SemaphoreType.DMA((COPIES,)),
             pltpu.SemaphoreType.DMA((COPIES,)),
         ],

time: 108 us -> 105 us (0.972)
  Pallas kernels: 102 us -> 99.6 us
    pallas_call x1, Pallas kernels: 102 us -> 99.6 us  [shards(): pl.pallas_call(window_kernel, out_shape=(jax.ShapeDtypeStruct((D, ENT), F...]
where the time goes in v6:
time: 105 us
  Pallas kernels  99.6 us (95%)
  local copies, waits for them, and re-layouts  4.41 us (4%)
    pallas_call x1, Pallas kernels, shards(): pl.pallas_call(window_kernel, out_shape=(jax.ShapeDtypeStruct((D, ENT), F...  99.6 us
    unnamed x10, local copies, waits for them, and re-layouts  4.41 us

profile of v6, /device:TPU:1, one launch (start us, length us, event | category | flops | bytes accessed | tf_op | source)
XLA Modules:
  0.0 104.6 jit_solution(3333805363433697729)
XLA Ops:
  0.6 99.6 %window.1 = (f32[200,1024]{1,0:T(8,128)}, f32[1,1024]{1,0:T(1,128)}, f32[200,1387]{1,0:T(8,128)}, f32[1387]{0:T(1024)}) custom-call(s32[2,128]{1,0:T(2,128)} %head_ids.1, s32[2,128]{1,0:T(2,128)} %rel_ids.1, s32[2,128]{1,0:T(2,128)} %tail_ids.1, s32[2,32]{1,0:T(2,128)} %neg_ids.1, f32[200,1024]{1,0:T(8,128)} %bitcast.14, f32[1,1024]{1,0:T(1,128)} %bitcast.16, ...), custom_call_target="tpu_custom_call" | custom-call | tf_op jit(solution)/shard_map/window/pallas_call | solution.py:507
  100.2 0.0 copy-start.2
  100.2 0.0 copy-start
  100.2 2.2 %copy.22 = f32[1024,200]{0,1:T(8,128)} copy(f32[1024,200]{0,1:T(8,128)} %bitcast.13) | data formatting | bytes 1638400
  102.4 0.0 copy-done.2
  102.4 0.6 copy.23
  103.0 0.0 copy-done
  103.0 0.0 copy-start.1
  103.0 1.0 copy.24
  104.0 0.0 copy-done.1
  104.0 0.6 copy.25
Async XLA Ops:
  100.2 2.2 %copy-start.2 = (f32[1,1024]{1,0:T(1,128)S(1)}, f32[1,1024]{1,0:T(1,128)}, u32[]{:S(2)}) copy-start(f32[1,1024]{1,0:T(1,128)} %get-tuple-element.9) | copy-start | bytes 12292
  100.2 2.8 %copy-start = (f32[200,1387]{1,0:T(8,128)S(1)}, f32[200,1387]{1,0:T(8,128)}, u32[]{:S(2)}) copy-start(f32[200,1387]{1,0:T(8,128)} %get-tuple-element.10) | copy-start | bytes 3328804
  103.0 1.0 copy-start.1

commit v7 on v6

--- a/solution.py
+++ b/solution.py
@@ -140,6 +140,14 @@
 def widen():
     row = lax.broadcasted_iota(jnp.int32, (D, LANES), 0)
     return jnp.where(row == lax.broadcasted_iota(jnp.int32, (D, LANES), 1), 1.0, 0.0).astype(BF16)
+
+
+def triples(first, last, body):
+    def three(j):
+        for k in range(3):
+            body(first + 3 * j + k)
+
+    loop(0, (last - first) // 3, three)
 
 
 def loop(first, last, body):
@@ -347,10 +355,10 @@
     pick_relations(0, own.rel[...].astype(BF16))
     wait_all(w_copies)
     own.acc[...] = jnp.zeros_like(own.acc)
-    loop(0, 5, forward)
+    triples(0, 6, forward)
     wait_all(along)
     near = negs_beside(0)
-    loop(5, STEPS, forward)
+    triples(6, STEPS, forward)
     near.wait()
     near = negs_to_mate(0)
     near.wait()
@@ -361,7 +369,7 @@
         more = r == 0
         if r == 1:
             own.acc[...] = jnp.zeros_like(own.acc)
-            loop(0, STEPS, lambda j: forward(j, own.slope))
+            triples(0, STEPS, lambda j: forward(j, own.slope))
             near.wait()
             tail_go.wait()
         pre2 = own.acc[...] + fc_bias[...]
@@ -381,11 +389,11 @@
         own.pre2_grad[...] = (query_grad * (sigma * (1.0 + pre2 * (1.0 - sigma)))).astype(BF16)
         own.grad_h[...] = jnp.zeros_like(own.grad_h)
         own.grad_r[...] = jnp.zeros_like(own.grad_r)
-        loop(0, 3, backward)
+        triples(0, 3, backward)
         b1_copy.wait()
         b.b2_send[...] = (b.neg_part[c, 1 - y_lo].astype(F32) + b.b1[1 - y_lo].astype(F32)).astype(BF16)
         b2_copy = copies.start(b.b2_send, b.b2_recv, beside)
-        loop(3, STEPS, backward)
+        triples(3, STEPS, backward)
         relation_grad = spread_nt_right(own.grad_r[...], space_ref[...])
         rel_row = rel_ids[r : r + 1, :]
         half = REL_PAD // 2
@@ -417,7 +425,7 @@
         b3_copies = [
             copies.start(b.b3_send.at[i], b.b3_recv.at[d], me.at(z=i)) for d, i in enumerate(zs)
         ]
-        loop(0, STEPS, backward_heads)
+        triples(0, STEPS, backward_heads)
         head_grad = spread_nt(space_ref[:D, :], own.grad_h[...])
         own.ent_grad[...] = spread_nt_right(head_grad, hot_rows(head_ids[r : r + 1, :], ENT))
         wait_all(b3_copies)
@@ -450,7 +458,6 @@
         if more:
             table = own.ent[...].astype(BF16)
             along, tail_go = rows_go(1, table)
-            pick_heads(1, table)
         s4_copies = []
         for h in range(2):
             wait_all(z_copies[h])
@@ -461,7 +468,8 @@
             slot = b.g_buf.at[h, c, me.x, me.y]
             s4_copies.append([copies.start(slot, slot, me.at(x=i, y=k)) for i, k in plane])
         if more:
-            loop(0, STEPS, forward_heads)
+            pick_heads(1, table)
+            triples(0, STEPS, forward_heads)
             wait_all(along)
             near = negs_beside(1)
         s6_copies = []

time: 105 us -> 102 us (0.971)
  Pallas kernels: 99.6 us -> 96.9 us
    pallas_call x1, Pallas kernels: 99.6 us -> 96.9 us  [shards(): pl.pallas_call(window_kernel, out_shape=(jax.ShapeDtypeStruct((D, ENT), F...]
where the time goes in v7:
time: 102 us
  Pallas kernels  96.9 us (95%)
  local copies, waits for them, and re-layouts  4.41 us (4%)
    pallas_call x1, Pallas kernels, shards(): pl.pallas_call(window_kernel, out_shape=(jax.ShapeDtypeStruct((D, ENT), F...  96.9 us
    unnamed x10, local copies, waits for them, and re-layouts  4.41 us

profile of v7, /device:TPU:1, one launch (start us, length us, event | category | flops | bytes accessed | tf_op | source)
XLA Modules:
  0.0 102.0 jit_solution(5920273475742869512)
XLA Ops:
  0.6 96.9 %window.1 = (f32[200,1024]{1,0:T(8,128)}, f32[1,1024]{1,0:T(1,128)}, f32[200,1387]{1,0:T(8,128)}, f32[1387]{0:T(1024)}) custom-call(s32[2,128]{1,0:T(2,128)} %head_ids.1, s32[2,128]{1,0:T(2,128)} %rel_ids.1, s32[2,128]{1,0:T(2,128)} %tail_ids.1, s32[2,32]{1,0:T(2,128)} %neg_ids.1, f32[200,1024]{1,0:T(8,128)} %bitcast.14, f32[1,1024]{1,0:T(1,128)} %bitcast.16, ...), custom_call_target="tpu_custom_call" | custom-call | tf_op jit(solution)/shard_map/window/pallas_call | solution.py:515
  97.5 0.0 copy-start.2
  97.6 0.0 copy-start
  97.6 2.2 %copy.22 = f32[1024,200]{0,1:T(8,128)} copy(f32[1024,200]{0,1:T(8,128)} %bitcast.13) | data formatting | bytes 1638400
  99.8 0.0 copy-done.2
  99.8 0.6 copy.23
  100.4 0.0 copy-done
  100.4 0.0 copy-start.1
  100.4 1.0 copy.24
  101.4 0.0 copy-done.1
  101.4 0.6 copy.25
Async XLA Ops:
  97.5 2.2 %copy-start.2 = (f32[1,1024]{1,0:T(1,128)S(1)}, f32[1,1024]{1,0:T(1,128)}, u32[]{:S(2)}) copy-start(f32[1,1024]{1,0:T(1,128)} %get-tuple-element.9) | copy-start | bytes 12292
  97.6 2.8 %copy-start = (f32[200,1387]{1,0:T(8,128)S(1)}, f32[200,1387]{1,0:T(8,128)}, u32[]{:S(2)}) copy-start(f32[200,1387]{1,0:T(8,128)} %get-tuple-element.10) | copy-start | bytes 3328804
  100.4 1.0 copy-start.1
